TPU v7x, 32 devices: a whole 2x2x4 slice. The times are simulated.
32 devices in a mesh: dp: 8 (over y, x, core), tensor: 4 (over z).
Axes of the slice: x: 2, y: 2, z: 4, core: 2. Of those that a mesh axis runs over, the one named last changes fastest.
Arguments:
- tokens: bfloat16 [8192, 1024], P(('dp', 'tensor')), may hold values from -6 to 6
- cotangent: bfloat16 [8192, 1024], P(('dp', 'tensor')), may hold values from -6 to 6
- gain_attn: float32 [1024], replicated, may hold values from 0.5 to 1.5
- gain_ffn: float32 [1024], replicated, may hold values from 0.5 to 1.5
- w_query: bfloat16 [1024, 1024], P('dp', 'tensor'), may hold values from -0.1875 to 0.1875
- w_key: bfloat16 [1024, 1024], P('dp', 'tensor'), may hold values from -0.1875 to 0.1875
- w_value: bfloat16 [1024, 2048], P('dp', 'tensor'), may hold values from -0.1875 to 0.1875
- w_gate_out: bfloat16 [1024, 2048], P('dp', 'tensor'), may hold values from -0.1875 to 0.1875
- w_decay: bfloat16 [1024, 8], P('dp', 'tensor'), may hold values from -0.1875 to 0.1875
- w_beta: bfloat16 [1024, 8], P('dp', 'tensor'), may hold values from -0.1875 to 0.1875
- w_output: bfloat16 [2048, 1024], P('tensor', 'dp'), may hold values from -0.125 to 0.125
- w_ffn_gate: bfloat16 [1024, 2816], P('dp', 'tensor'), may hold values from -0.1875 to 0.1875
- w_ffn_up: bfloat16 [1024, 2816], P('dp', 'tensor'), may hold values from -0.1875 to 0.1875
- w_ffn_down: bfloat16 [2816, 1024], P('tensor', 'dp'), may hold values from -0.109375 to 0.109375
- conv_query: float32 [4, 1024], replicated, may hold values from -3 to 3
- conv_key: float32 [4, 1024], replicated, may hold values from -3 to 3
- conv_value: float32 [4, 2048], replicated, may hold values from -3 to 3
- a_log: float32 [8], replicated, may hold values from -2.5 to 1
- dt_bias: float32 [8], replicated, may hold values from -4 to -1
- out_gain: float32 [256], replicated, may hold values from 0.5 to 1.5
Outputs:
- output: bfloat16 [8192, 1024], P(('dp', 'tensor'))
- grad_tokens: float32 [8192, 1024], P(('dp', 'tensor'))
- grad_gain_attn: float32 [1024], replicated
- grad_gain_ffn: float32 [1024], replicated
- grad_w_query: float32 [1024, 1024], P('dp', 'tensor')
- grad_w_key: float32 [1024, 1024], P('dp', 'tensor')
- grad_w_value: float32 [1024, 2048], P('dp', 'tensor')
- grad_w_gate_out: float32 [1024, 2048], P('dp', 'tensor')
- grad_w_decay: float32 [1024, 8], P('dp', 'tensor')
- grad_w_beta: float32 [1024, 8], P('dp', 'tensor')
- grad_w_output: float32 [2048, 1024], P('tensor', 'dp')
- grad_w_ffn_gate: float32 [1024, 2816], P('dp', 'tensor')
- grad_w_ffn_up: float32 [1024, 2816], P('dp', 'tensor')
- grad_w_ffn_down: float32 [2816, 1024], P('tensor', 'dp')
- grad_conv_query: float32 [4, 1024], replicated
- grad_conv_key: float32 [4, 1024], replicated
- grad_conv_value: float32 [4, 2048], replicated
- grad_a_log: float32 [8], replicated
- grad_dt_bias: float32 [8], replicated
- grad_out_gain: float32 [256], replicated
All inputs are finite; a program needn't handle non-finite values.
Results may differ from a plain program's by a relative error of at most 0.017.
Values may be sent and summed in bfloat16 or wider, within the bound.
No kernel may reach another device: no remote copies, remote signals or barrier semaphores. Data moves between devices by JAX's collectives and lax.ppermute only.
A program may use at most 192 MiB of HBM per device.

v0:
```python
import jax
import jax.numpy as jnp
from jax import lax
from jax.sharding import PartitionSpec as P

DK = 128
DV = 256
CONV = 4
SPAN = 64
SEQ_LEN = 1024


PRECISE = lax.Precision.HIGHEST


def rms_norm(values, gain):
    return values * lax.rsqrt(jnp.mean(values * values, -1, keepdims=True) + 1e-05) * gain


def swiglu_act(gate_val, up_val):
    return jax.nn.silu(gate_val) * up_val


def matmul_tn(left, right):
    return lax.dot_general(
        left, right, (((0,), (0,)), ((), ())), preferred_element_type=jnp.float32
    )


def matmul_nt(left, right):
    return lax.dot_general(
        left, right, (((1,), (1,)), ((), ())), preferred_element_type=jnp.float32
    )


def place_cols(member, width, offset):
    blank = jnp.zeros(member.shape[:-1] + (width,), jnp.float32)
    return lax.dynamic_update_slice_in_dim(blank, member, offset, member.ndim - 1)


def conv_silu(pre_conv, taps):
    length = pre_conv.shape[1]
    padded = jnp.pad(pre_conv, ((0, 0), (CONV - 1, 0), (0, 0)))
    summed = padded[:, 0:length, :] * taps[0]
    for offset in range(1, CONV):
        summed = summed + padded[:, offset : offset + length, :] * taps[offset]
    return jax.nn.silu(summed)


def split_heads(values, width):
    seq_count = values.shape[0]
    return values.reshape(seq_count, SEQ_LEN // SPAN, SPAN, -1, width).transpose(0, 1, 3, 2, 4)


def per_head(values, seq_count):
    return values.reshape(seq_count, SEQ_LEN // SPAN, SPAN, -1).transpose(0, 1, 3, 2)


def span_step(carried, pieces):
    queries, key_rows, w_rows, u_rows, cumulative, inner_mix = pieces
    new_values = u_rows - jnp.einsum("shcd,shde->shce", w_rows, carried, precision=PRECISE)
    outcome = jnp.exp(cumulative)[..., None] * jnp.einsum(
        "shcd,shde->shce", queries, carried, precision=PRECISE
    )
    outcome = outcome + jnp.einsum("shij,shje->shie", inner_mix, new_values, precision=PRECISE)
    final_log = cumulative[..., -1]
    weighted = key_rows * jnp.exp(final_log[..., None] - cumulative)[..., None]
    carried = jnp.exp(final_log)[..., None, None] * carried + jnp.einsum(
        "shcd,shce->shde", weighted, new_values, precision=PRECISE
    )
    return (carried, outcome)


def delta_mixer(
    q_pre, k_pre, v_pre, o_pre, a_pre, b_pre, conv_q, conv_k, conv_v, a_log, dt_bias, out_gain
):
    token_count = q_pre.shape[0]
    head_count = a_pre.shape[1]
    seq_count = token_count // SEQ_LEN
    queries = split_heads(conv_silu(q_pre.reshape(seq_count, SEQ_LEN, -1), conv_q), DK)
    queries = (
        queries * lax.rsqrt(jnp.sum(queries * queries, -1, keepdims=True) + 1e-06) * DK ** (-0.5)
    )
    key_rows = split_heads(conv_silu(k_pre.reshape(seq_count, SEQ_LEN, -1), conv_k), DK)
    key_rows = key_rows * lax.rsqrt(jnp.sum(key_rows * key_rows, -1, keepdims=True) + 1e-06)
    value_rows = split_heads(conv_silu(v_pre.reshape(seq_count, SEQ_LEN, -1), conv_v), DV)
    beta_rows = per_head(jax.nn.sigmoid(b_pre), seq_count)
    log_decay = per_head(-jnp.exp(a_log) * jax.nn.softplus(a_pre + dt_bias), seq_count)
    cumulative = jnp.cumsum(log_decay, axis=-1)
    row_ids = lax.broadcasted_iota(jnp.int32, (SPAN, SPAN), 0)
    col_ids = lax.broadcasted_iota(jnp.int32, (SPAN, SPAN), 1)
    causal = row_ids >= col_ids
    strict = (row_ids > col_ids).astype(jnp.float32)
    differ = cumulative[..., :, None] - cumulative[..., None, :]
    decays = jnp.exp(jnp.where(causal, differ, 0.0)) * causal.astype(jnp.float32)
    lower_mat = (
        beta_rows[..., :, None]
        * jnp.einsum("snhid,snhjd->snhij", key_rows, key_rows, precision=PRECISE)
        * decays
        * strict
    )
    identity = jnp.eye(SPAN, dtype=jnp.float32)
    inverse = identity - lower_mat
    powered = lower_mat
    for repeat in range(SPAN.bit_length() - 2):
        powered = jnp.einsum("snhij,snhjk->snhik", powered, powered, precision=PRECISE)
        inverse = jnp.einsum("snhij,snhjk->snhik", inverse, identity + powered, precision=PRECISE)
    w_rows = jnp.einsum(
        "snhij,snhjd->snhid",
        inverse,
        (beta_rows * jnp.exp(cumulative))[..., None] * key_rows,
        precision=PRECISE,
    )
    u_rows = jnp.einsum(
        "snhij,snhjd->snhid", inverse, beta_rows[..., None] * value_rows, precision=PRECISE
    )
    inner_mix = jnp.einsum("snhid,snhjd->snhij", queries, key_rows, precision=PRECISE) * decays
    by_block = tuple(
        (
            member.swapaxes(0, 1)
            for member in (queries, key_rows, w_rows, u_rows, cumulative, inner_mix)
        )
    )
    start_state = jnp.zeros((seq_count, head_count, DK, DV), jnp.float32)
    final_state, outcome = lax.scan(jax.checkpoint(span_step), start_state, by_block)
    core_out = outcome.transpose(1, 0, 3, 2, 4).reshape(seq_count, SEQ_LEN, head_count, DV)
    gate_rows = o_pre.reshape(seq_count, SEQ_LEN, head_count, DV)
    normed = (
        core_out
        * lax.rsqrt(jnp.mean(core_out * core_out, -1, keepdims=True) + 1e-05)
        * out_gain
        * jax.nn.silu(gate_rows)
    )
    return normed.reshape(token_count, head_count * DV)


def local(
    tokens,
    cotangent,
    gain_attn,
    gain_ffn,
    w_query,
    w_key,
    w_value,
    w_gate_out,
    w_decay,
    w_beta,
    w_output,
    w_ffn_gate,
    w_ffn_up,
    w_ffn_down,
    conv_query,
    conv_key,
    conv_value,
    a_log,
    dt_bias,
    out_gain,
):
    gathered = (
        lax.all_gather(w_query, "dp", axis=0, tiled=True),
        lax.all_gather(w_key, "dp", axis=0, tiled=True),
        lax.all_gather(w_value, "dp", axis=0, tiled=True),
        lax.all_gather(w_gate_out, "dp", axis=0, tiled=True),
        lax.all_gather(w_decay, "dp", axis=0, tiled=True),
        lax.all_gather(w_beta, "dp", axis=0, tiled=True),
        lax.all_gather(w_output, "dp", axis=1, tiled=True),
        lax.all_gather(w_ffn_gate, "dp", axis=0, tiled=True),
        lax.all_gather(w_ffn_up, "dp", axis=0, tiled=True),
        lax.all_gather(w_ffn_down, "dp", axis=1, tiled=True),
    )
    position = lax.axis_index("tensor")
    head_count = w_decay.shape[1]
    key_width = head_count * DK
    value_width = head_count * DV
    taps_query = lax.dynamic_slice_in_dim(conv_query, position * key_width, key_width, 1)
    taps_key = lax.dynamic_slice_in_dim(conv_key, position * key_width, key_width, 1)
    taps_value = lax.dynamic_slice_in_dim(conv_value, position * value_width, value_width, 1)
    log_scale = lax.dynamic_slice_in_dim(a_log, position * head_count, head_count, 0)
    bias_heads = lax.dynamic_slice_in_dim(dt_bias, position * head_count, head_count, 0)
    tok_rows = tokens.astype(jnp.float32)
    normed_one, norm_one_pull = jax.vjp(rms_norm, tok_rows, gain_attn)
    mixer_in = lax.all_gather(normed_one.astype(jnp.bfloat16), "tensor", axis=0, tiled=True)
    projected = [
        jnp.dot(mixer_in, gathered[index_w], preferred_element_type=jnp.float32)
        for index_w in range(6)
    ]
    mixed, mixer_pull = jax.vjp(
        delta_mixer,
        projected[0],
        projected[1],
        projected[2],
        projected[3],
        projected[4],
        projected[5],
        taps_query,
        taps_key,
        taps_value,
        log_scale,
        bias_heads,
        out_gain,
    )
    mixed_low = mixed.astype(jnp.bfloat16)
    branch = lax.psum_scatter(
        jnp.dot(mixed_low, gathered[6], preferred_element_type=jnp.float32),
        "tensor",
        scatter_dimension=0,
        tiled=True,
    )
    middle = tok_rows + branch
    normed_two, norm_two_pull = jax.vjp(rms_norm, middle, gain_ffn)
    ffn_in = lax.all_gather(normed_two.astype(jnp.bfloat16), "tensor", axis=0, tiled=True)
    gate_val = jnp.dot(ffn_in, gathered[7], preferred_element_type=jnp.float32)
    up_val = jnp.dot(ffn_in, gathered[8], preferred_element_type=jnp.float32)
    activated, swiglu_pull = jax.vjp(swiglu_act, gate_val, up_val)
    activated_low = activated.astype(jnp.bfloat16)
    ffn_out = lax.psum_scatter(
        jnp.dot(activated_low, gathered[9], preferred_element_type=jnp.float32).astype(
            jnp.bfloat16
        ),
        "tensor",
        scatter_dimension=0,
        tiled=True,
    ).astype(jnp.float32)
    output = (middle + ffn_out).astype(jnp.bfloat16)
    weights_back = (
        lax.all_gather(w_query, "dp", axis=0, tiled=True),
        lax.all_gather(w_key, "dp", axis=0, tiled=True),
        lax.all_gather(w_value, "dp", axis=0, tiled=True),
        lax.all_gather(w_gate_out, "dp", axis=0, tiled=True),
        lax.all_gather(w_decay, "dp", axis=0, tiled=True),
        lax.all_gather(w_beta, "dp", axis=0, tiled=True),
        lax.all_gather(w_output, "dp", axis=1, tiled=True),
        lax.all_gather(w_ffn_gate, "dp", axis=0, tiled=True),
        lax.all_gather(w_ffn_up, "dp", axis=0, tiled=True),
        lax.all_gather(w_ffn_down, "dp", axis=1, tiled=True),
    )
    cot_rows = lax.all_gather(cotangent, "tensor", axis=0, tiled=True)
    d_activated = matmul_nt(cot_rows, weights_back[9])
    d_gate, d_up = swiglu_pull(d_activated)
    d_gate_low = d_gate.astype(jnp.bfloat16)
    d_up_low = d_up.astype(jnp.bfloat16)
    grad_down = matmul_tn(activated_low, cot_rows)
    grad_fgate = matmul_tn(ffn_in, d_gate_low)
    grad_fup = matmul_tn(ffn_in, d_up_low)
    d_ffn_in = matmul_nt(d_gate_low, weights_back[7]) + matmul_nt(d_up_low, weights_back[8])
    d_normed_two = lax.psum_scatter(
        d_ffn_in.astype(jnp.bfloat16), "tensor", scatter_dimension=0, tiled=True
    ).astype(jnp.float32)
    d_middle_norm, d_gain_ffn = norm_two_pull(d_normed_two)
    d_middle = cotangent.astype(jnp.float32) + d_middle_norm
    branch_cot = lax.all_gather(d_middle.astype(jnp.bfloat16), "tensor", axis=0, tiled=True)
    d_mixed = matmul_nt(branch_cot, weights_back[6])
    grad_out = matmul_tn(mixed_low, branch_cot)
    mixer_grads = mixer_pull(d_mixed)
    d_proj = [mixer_grads[index_w].astype(jnp.bfloat16) for index_w in range(6)]
    grad_proj = [matmul_tn(mixer_in, d_proj[index_w]) for index_w in range(6)]
    d_mixer_in = matmul_nt(d_proj[0], weights_back[0])
    for index_w in range(1, 6):
        d_mixer_in = d_mixer_in + matmul_nt(d_proj[index_w], weights_back[index_w])
    d_normed_one = lax.psum_scatter(
        d_mixer_in.astype(jnp.bfloat16), "tensor", scatter_dimension=0, tiled=True
    ).astype(jnp.float32)
    d_tok_norm, d_gain_attn = norm_one_pull(d_normed_one)
    grad_tokens = d_middle + d_tok_norm
    summed = (
        lax.psum_scatter(
            grad_proj[0].astype(jnp.bfloat16), "dp", scatter_dimension=0, tiled=True
        ).astype(jnp.float32),
        lax.psum_scatter(
            grad_proj[1].astype(jnp.bfloat16), "dp", scatter_dimension=0, tiled=True
        ).astype(jnp.float32),
        lax.psum_scatter(
            grad_proj[2].astype(jnp.bfloat16), "dp", scatter_dimension=0, tiled=True
        ).astype(jnp.float32),
        lax.psum_scatter(
            grad_proj[3].astype(jnp.bfloat16), "dp", scatter_dimension=0, tiled=True
        ).astype(jnp.float32),
        lax.psum_scatter(
            grad_proj[4].astype(jnp.bfloat16), "dp", scatter_dimension=0, tiled=True
        ).astype(jnp.float32),
        lax.psum_scatter(
            grad_proj[5].astype(jnp.bfloat16), "dp", scatter_dimension=0, tiled=True
        ).astype(jnp.float32),
        lax.psum_scatter(
            grad_out.astype(jnp.bfloat16), "dp", scatter_dimension=1, tiled=True
        ).astype(jnp.float32),
        lax.psum_scatter(
            grad_fgate.astype(jnp.bfloat16), "dp", scatter_dimension=0, tiled=True
        ).astype(jnp.float32),
        lax.psum_scatter(
            grad_fup.astype(jnp.bfloat16), "dp", scatter_dimension=0, tiled=True
        ).astype(jnp.float32),
        lax.psum_scatter(
            grad_down.astype(jnp.bfloat16), "dp", scatter_dimension=1, tiled=True
        ).astype(jnp.float32),
    )
    small_sums = lax.psum(
        (
            d_gain_attn,
            d_gain_ffn,
            place_cols(mixer_grads[6], conv_query.shape[1], position * key_width),
            place_cols(mixer_grads[7], conv_key.shape[1], position * key_width),
            place_cols(mixer_grads[8], conv_value.shape[1], position * value_width),
            place_cols(mixer_grads[9], a_log.shape[0], position * head_count),
            place_cols(mixer_grads[10], dt_bias.shape[0], position * head_count),
            mixer_grads[11],
        ),
        ("dp", "tensor"),
    )
    return (
        output,
        grad_tokens,
        small_sums[0],
        small_sums[1],
        summed[0],
        summed[1],
        summed[2],
        summed[3],
        summed[4],
        summed[5],
        summed[6],
        summed[7],
        summed[8],
        summed[9],
        small_sums[2],
        small_sums[3],
        small_sums[4],
        small_sums[5],
        small_sums[6],
        small_sums[7],
    )


def solution(mesh):
    placed = (
        P(("dp", "tensor"), None),
        P(("dp", "tensor"), None),
        P(),
        P(),
        P("dp", "tensor"),
        P("dp", "tensor"),
        P("dp", "tensor"),
        P("dp", "tensor"),
        P("dp", "tensor"),
        P("dp", "tensor"),
        P("tensor", "dp"),
        P("dp", "tensor"),
        P("dp", "tensor"),
        P("tensor", "dp"),
        P(),
        P(),
        P(),
        P(),
        P(),
        P(),
    )
    return jax.shard_map(
        local,
        mesh=mesh,
        in_specs=placed,
        out_specs=(
            P(("dp", "tensor"), None),
            P(("dp", "tensor"), None),
            P(),
            P(),
            P("dp", "tensor"),
            P("dp", "tensor"),
            P("dp", "tensor"),
            P("dp", "tensor"),
            P("dp", "tensor"),
            P("dp", "tensor"),
            P("tensor", "dp"),
            P("dp", "tensor"),
            P("dp", "tensor"),
            P("tensor", "dp"),
            P(),
            P(),
            P(),
            P(),
            P(),
            P(),
        ),
        check_vma=False,
    )
```

profile of v0, /device:TPU:1, one launch (start us, length us, event | category | flops | bytes accessed | tf_op | source)
XLA Modules:
  0.0 1524.3 jit_solution(9945732094442232604)
XLA Ops:
  13.4 11.2 all_gather.54
  24.8 8.7 all_gather.53
  33.5 8.5 all_gather.55
  42.0 11.1 all_gather.57
  63.3 3.4 fusion.162
  70.0 5.1 fusion.255
  77.6 3.7 fusion.265
  83.9 3.7 fusion.266
  90.1 3.7 fusion.267
  99.8 3.6 fusion.152
  106.1 2.9 convolution_add_fusion.4
  109.0 3.3 fusion.188
  114.9 3.2 fusion.85
  118.1 2.7 reshape.1198
  120.9 4.1 fusion.185
  132.6 2.6 convolution_bitcast_fusion.26
  135.2 3.4 fusion.88
  141.2 116.1 %while.42 = (s32[]{:T(128)}, f32[1,2,128,256]{3,2,1,0:T(8,128)S(1)}, f32[16,1,2,64,256]{4,3,2,1,0:T(8,128)S(1)}, f32[16,1,2,128,256]{4,3,2,1,0:T(8,128)}, f32[16...) while((s32[]{:T(128)}, ...), condition=%wide.region_5.6_spmd.clone, body=%wide.region_4.5_spmd.clone.sunk | while | flops 176668800 | bytes 2759866 | solution.py:125
  266.1 6.4 multiply_convert_fusion.2
  272.5 4.8 fusion.271
  278.0 75.1 %reduce-scatter.27.cloned.1.call-done = f32[256,1024]{1,0:T(8,128)} async-done(((f32[1024,1024]{1,0:T(8,128)}), f32[256,1024]{1,0:T(8,128)}) %reduce-scatter.27.cloned.1.call-update) | async-done | bytes 1048592 | tf_op jit(solution)/shard_map/reduce_scatter | solution.py:203
  358.7 22.5 %all-gather.21.cloned.1.call-done = bf16[1024,704]{0,1:T(8,128)(2,1)} async-done(((bf16[128,704]{0,1:T(8,128)(2,1)}), bf16[1024,704]{0,1:T(8,128)(2,1)}) %all-gather.21.cloned.1.call-update) | async-done | bytes 1441808 | tf_op jit(solution)/shard_map/all_gather | solution.py:167
  381.2 47.2 %all-gather.19.cloned.1.call-done = bf16[1024,1024]{1,0:T(8,128)(2,1)} async-done(((bf16[256,1024]{1,0:T(8,128)(2,1)}), bf16[1024,1024]{1,0:T(8,128)(2,1)}) %all-gather.19.cloned.1.call-update) | async-done | bytes 2097168 | tf_op jit(solution)/shard_map/all_gather | solution.py:211
  428.5 5.3 fusion.272
  433.8 21.2 %all-gather.23.cloned.1.call-done = bf16[1024,704]{0,1:T(8,128)(2,1)} async-done(((bf16[128,704]{0,1:T(8,128)(2,1)}), bf16[1024,704]{0,1:T(8,128)(2,1)}) %all-gather.23.cloned.1.call-update) | async-done | bytes 1441808 | tf_op jit(solution)/shard_map/all_gather | solution.py:168
  455.0 5.3 fusion.273
  460.3 21.8 %all-gather.25.cloned.1.call-done = bf16[704,1024]{1,0:T(8,128)(2,1)} async-done(((bf16[704,128]{1,0:T(8,128)(2,1)}), bf16[704,1024]{1,0:T(8,128)(2,1)}) %all-gather.25.cloned.1.call-update) | async-done | bytes 1441808 | tf_op jit(solution)/shard_map/all_gather | solution.py:169
  482.1 46.5 %all-gather.27.cloned.1.call-done = bf16[1024,1024]{1,0:T(8,128)(2,1)} async-done(((bf16[256,1024]{1,0:T(8,128)(2,1)}), bf16[1024,1024]{1,0:T(8,128)(2,1)}) %all-gather.27.cloned.1.call-update) | async-done | bytes 2097168 | tf_op jit(solution)/shard_map/all_gather | solution.py:237
  528.6 7.7 multiply_convert_fusion
  538.7 3.2 add_convert_fusion.1
  542.0 42.3 %reduce-scatter.31.cloned.1.call-done = bf16[256,1024]{1,0:T(8,128)(2,1)} async-done(((bf16[1024,1024]{1,0:T(8,128)(2,1)}), bf16[256,1024]{1,0:T(8,128)(2,1)}) %reduce-scatter.31.cloned.1.call-update) | async-done | bytes 524304 | tf_op jit(solution)/shard_map/reduce_scatter | solution.py:246
  589.1 4.8 convolution_convert_fusion.2
  596.8 5.0 convolution_convert_fusion.1
  604.5 3.5 reshape.1206
  608.0 4.8 convolution_convert_fusion.3
  615.5 18.8 %all-gather.29.cloned.1.call-done = bf16[1024,1024]{1,0:T(8,128)(2,1)} async-done(((bf16[256,1024]{1,0:T(8,128)(2,1)}), bf16[1024,1024]{1,0:T(8,128)(2,1)}) %all-gather.29.cloned.1.call-update) | async-done | bytes 2097168 | tf_op jit(solution)/shard_map/all_gather | solution.py:251
  634.3 7.3 fusion.75
  641.6 3.6 reshape.1205
  645.2 3.8 multiply_reduce_fusion.2
  657.6 291.4 %while.43 = (s32[]{:T(128)}, f32[1,2,128,256]{2,3,1,0:T(8,128)S(1)}, f32[16,1,2,64,128]{4,3,2,1,0:T(8,128)}, f32[16,1,2,64,128]{4,3,2,1,0:T(8,128)}, f32[16,1,2,...) while((s32[]{:T(128)}, ...), condition=%wide.region_18.19_spmd.clone, body=%wide.region_13.18_spmd.clone.sunk | while | flops 453706624 | bytes 8629691 | solution.py:125
  949.0 3.2 convolution_bitcast_fusion.25
  986.3 3.9 fusion.140
  999.4 3.1 reshape.1215
  1004.1 5.8 fusion.77
  1019.8 2.7 fusion.150
  1031.8 3.1 copy.353
  1034.9 3.0 reshape.1207
  1045.9 3.0 copy.384
  1048.9 3.9 reshape.1216
  1052.8 3.2 convolution_convert_fusion.4
  1057.4 5.9 multiply_reduce_fusion.5
  1069.2 3.9 fusion.278
  1073.0 2.8 fusion.275
  1086.0 2.7 add_convert_fusion
  1090.1 4.5 convolution_convert_fusion
  1103.9 25.2 %reduce-scatter.37.cloned.1.call-done = bf16[128,256]{1,0:T(8,128)(2,1)} async-done(((bf16[1024,256]{1,0:T(8,128)(2,1)}), bf16[128,256]{1,0:T(8,128)(2,1)}) %reduce-scatter.37.cloned.1.call-update) | async-done | bytes 65552 | tf_op jit(solution)/shard_map/reduce_scatter | solution.py:269
  1130.6 35.7 %reduce-scatter.35.cloned.1.call-done = bf16[128,256]{1,0:T(8,128)(2,1)} async-done(((bf16[1024,256]{1,0:T(8,128)(2,1)}), bf16[128,256]{1,0:T(8,128)(2,1)}) %reduce-scatter.35.cloned.1.call-update) | async-done | bytes 65552 | tf_op jit(solution)/shard_map/reduce_scatter | solution.py:266
  1167.8 37.7 %reduce-scatter.47.cloned.1.call-done = bf16[128,512]{1,0:T(8,128)(2,1)} async-done(((bf16[1024,512]{1,0:T(8,128)(2,1)}), bf16[128,512]{1,0:T(8,128)(2,1)}) %reduce-scatter.47.cloned.1.call-update) | async-done | bytes 131088
  1207.2 37.4 %reduce-scatter.39.cloned.1.call-done = bf16[128,512]{1,0:T(8,128)(2,1)} async-done(((bf16[1024,512]{1,0:T(8,128)(2,1)}), bf16[128,512]{1,0:T(8,128)(2,1)}) %reduce-scatter.39.cloned.1.call-update) | async-done | bytes 131088 | tf_op jit(solution)/shard_map/reduce_scatter | solution.py:272
  1246.3 37.5 %reduce-scatter.41.cloned.1.call-done = bf16[128,512]{1,0:T(8,128)(2,1)} async-done(((bf16[1024,512]{1,0:T(8,128)(2,1)}), bf16[128,512]{1,0:T(8,128)(2,1)}) %reduce-scatter.41.cloned.1.call-update) | async-done | bytes 131088 | tf_op jit(solution)/shard_map/reduce_scatter | solution.py:275
  1285.5 44.3 %reduce-scatter.33.cloned.1.call-done = bf16[256,1024]{1,0:T(8,128)(2,1)} async-done(((bf16[1024,1024]{1,0:T(8,128)(2,1)}), bf16[256,1024]{1,0:T(8,128)(2,1)}) %reduce-scatter.33.cloned.1.call-update) | async-done | bytes 524304 | tf_op jit(solution)/shard_map/reduce_scatter | solution.py:260
  1332.0 42.8 %reduce-scatter.29.cloned.1.call-done = bf16[256,1024]{1,0:T(8,128)(2,1)} async-done(((bf16[1024,1024]{1,0:T(8,128)(2,1)}), bf16[256,1024]{1,0:T(8,128)(2,1)}) %reduce-scatter.29.cloned.1.call-update) | async-done | bytes 524304 | tf_op jit(solution)/shard_map/reduce_scatter | solution.py:216
  1374.8 2.9 fusion.134
  1377.7 129.7 %all-reduce.31.cloned.1.call-done = (f32[1024]{0:T(1024)}, f32[1024]{0:T(1024)}, f32[4,1024]{1,0:T(4,128)}, f32[4,1024]{1,0:T(4,128)}, f32[4,2048]{1,0:T(4,128)}, /*index=5*/f32[8]{0:T(128)}, f32[8]{0:T(128)}, f32[256]{0:T(256)}) async-done(((f32[1024]{0:T(1024)}, f32[1024]{0:T(1024)}, f32[4,1024]{1,0:T(4,128)}, f32[4,1024]{1,0:T(4,128)}, f32[4,2048]{1,0:T(4,128)}, /*index=5*/f32[8]{0:T(128)}, f32[8]{0:T(128)}, ...) | async-done | bytes 74832 | tf_op jit(solution)/shard_map/psum | solution.py:297
  (1199 shorter events, 611.6 us)
Async XLA Ops:
  7.2 17.4 %copy-start.150 = (f32[8]{0:T(128)S(1)}, f32[8]{0:T(128)}, u32[]{:S(2)}) copy-start(f32[8]{0:T(128)} %param.41) | copy-start | bytes 100
  7.2 17.5 %copy-start.156 = (f32[8]{0:T(128)S(1)}, f32[8]{0:T(128)}, u32[]{:S(2)}) copy-start(f32[8]{0:T(128)} %param.42) | copy-start | bytes 100
  7.2 17.6 %copy-start.148 = (bf16[128,2]{0,1:T(2,128)(2,1)S(1)}, bf16[128,2]{0,1:T(2,128)(2,1)}, u32[]{:S(2)}) copy-start(bf16[128,2]{0,1:T(2,128)(2,1)} %param.32) | copy-start | bytes 1540
  7.2 26.3 %copy-start.149 = (bf16[128,2]{0,1:T(2,128)(2,1)S(1)}, bf16[128,2]{0,1:T(2,128)(2,1)}, u32[]{:S(2)}) copy-start(bf16[128,2]{0,1:T(2,128)(2,1)} %param.33) | copy-start | bytes 1540
  7.2 34.8 %copy-start.97 = (bf16[128,256]{1,0:T(8,128)(2,1)S(1)}, bf16[128,256]{1,0:T(8,128)(2,1)}, u32[]{:S(2)}) copy-start(bf16[128,256]{1,0:T(8,128)(2,1)} %param.28) | copy-start | bytes 196612
  7.3 45.8 %copy-start.141 = (f32[256]{0:T(256)S(1)}, f32[256]{0:T(256)}, u32[]{:S(2)}) copy-start(f32[256]{0:T(256)} %param.43) | copy-start | bytes 3076
  7.3 51.1 %all-gather.11.cloned.1.call-start = ((), (), s32[]{:S(2)}) async-start(), calls=%async_computation.14 | async-start | bytes 2621440 | tf_op jit(solution)/shard_map/all_gather | solution.py:182
  8.6 48.1 %copy-start.139 = (f32[256]{0:T(256)}, f32[256]{0:T(256)S(1)}, u32[]{:S(2)}) copy-start(f32[256]{0:T(256)S(1)} %fusion.135) | copy-start | bytes 3076
  8.6 48.1 %copy-start.119 = (f32[256]{0:T(256)}, f32[256]{0:T(256)S(1)}, u32[]{:S(2)}) copy-start(f32[256]{0:T(256)S(1)} %fusion.244) | copy-start | bytes 3076
  10.6 101.7 %all-gather.13.cloned.1.call-start = ((), (), s32[]{:S(2)}) async-start(), calls=%async_computation.15 | async-start | bytes 1179648 | tf_op jit(solution)/shard_map/all_gather | solution.py:162
  11.4 254.7 %all-gather.15.cloned.1.call-start = ((), (), s32[]{:S(2)}) async-start(), calls=%async_computation.16 | async-start | bytes 1179648 | tf_op jit(solution)/shard_map/all_gather | solution.py:163
  12.1 260.4 %all-gather.17.cloned.1.call-start = ((), (), s32[]{:S(2)}) async-start(), calls=%async_computation.17 | async-start | bytes 1179648 | tf_op jit(solution)/shard_map/all_gather | solution.py:166
  12.7 340.3 %reduce-scatter.27.cloned.1.call-start = ((), (), s32[]{:S(2)}) async-start(), calls=%async_computation.18 | async-start | bytes 5242880 | tf_op jit(solution)/shard_map/reduce_scatter | solution.py:203
  12.8 115.1 %copy-start.50 = (f32[64,64]{0,1:T(8,128)}, f32[64,64]{0,1:T(8,128)S(1)}, u32[]{:S(2)}) copy-start(f32[64,64]{0,1:T(8,128)S(1)} %get-tuple-element.769) | copy-start | bytes 49156
  12.8 125.8 %copy-start.59 = (f32[64,64]{0,1:T(8,128)}, f32[64,64]{0,1:T(8,128)S(1)}, u32[]{:S(2)}) copy-start(f32[64,64]{0,1:T(8,128)S(1)} %get-tuple-element.770) | copy-start | bytes 49156
  13.4 125.2 %copy-start.74 = (pred[64,64]{0,1:T(8,128)(4,1)}, pred[64,64]{0,1:T(8,128)(4,1)S(1)}, u32[]{:S(2)}) copy-start(pred[64,64]{0,1:T(8,128)(4,1)S(1)} %get-tuple-element.767) | copy-start | bytes 12292
  24.6 36.1 %copy-start.65 = (bf16[1024,256]{1,0:T(8,128)(2,1)}, bf16[1024,256]{1,0:T(8,128)(2,1)S(1)}, u32[]{:S(2)}) copy-start(bf16[1024,256]{1,0:T(8,128)(2,1)S(1)} %all_gather.54) | copy-start | bytes 1572868
  24.7 42.0 %copy-start.144 = (f32[2]{0:T(128)}, f32[2]{0:T(128)S(1)}, u32[]{:S(2)}) copy-start(f32[2]{0:T(128)S(1)} %fusion.246) | copy-start | bytes 28
  33.5 33.2 %copy-start.105 = (bf16[1024,2]{0,1:T(2,128)(2,1)}, bf16[1024,2]{0,1:T(2,128)(2,1)S(1)}, u32[]{:S(2)}) copy-start(bf16[1024,2]{0,1:T(2,128)(2,1)S(1)} %all_gather.53) | copy-start | bytes 12292
  63.3 69.2 %copy-start.68 = (f32[16,2,64]{2,1,0:T(2,128)}, f32[16,2,64]{2,1,0:T(2,128)S(1)}, u32[]{:S(2)}) copy-start(f32[16,2,64]{2,1,0:T(2,128)S(1)} %add_rsqrt_fusion.1) | copy-start | bytes 24580
  69.9 7.7 copy-start.93
  70.0 23.9 %copy-start.78 = (f32[1,16,64,2]{2,1,3,0:T(8,128)}, f32[1,16,64,2]{2,1,3,0:T(8,128)S(1)}, u32[]{:S(2)}) copy-start(f32[1,16,64,2]{2,1,3,0:T(8,128)S(1)} %reshape.1195) | copy-start | bytes 24580
  70.0 65.2 %copy-start.70 = (f32[16,2,64]{2,1,0:T(2,128)}, f32[16,2,64]{2,1,0:T(2,128)S(1)}, u32[]{:S(2)}) copy-start(f32[16,2,64]{2,1,0:T(2,128)S(1)} %copy.308) | copy-start | bytes 24580
  112.3 20.3 %copy-start.87 = (f32[16,2,64]{2,1,0:T(2,128)}, f32[16,2,64]{2,1,0:T(2,128)S(1)}, u32[]{:S(2)}) copy-start(f32[16,2,64]{2,1,0:T(2,128)S(1)} %copy.326) | copy-start | bytes 24580
  120.9 14.3 copy-start.9
  277.4 78.3 %copy-start.102 = (f32[1024]{0:T(1024)S(1)}, f32[1024]{0:T(1024)}, u32[]{:S(2)}) copy-start(f32[1024]{0:T(1024)} %param.27) | copy-start | bytes 12292
  277.4 103.9 %all-gather.21.cloned.1.call-start = ((), (), s32[]{:S(2)}) async-start(), calls=%async_computation.20 | async-start | bytes 1622016 | tf_op jit(solution)/shard_map/all_gather | solution.py:167
  277.9 150.5 %all-gather.19.cloned.1.call-start = ((), (), s32[]{:S(2)}) async-start(), calls=%async_computation.19 | async-start | bytes 2621440 | tf_op jit(solution)/shard_map/all_gather | solution.py:211
  354.6 232.0 %copy-start.109 = (f32[256]{0:T(256)}, f32[256]{0:T(256)S(1)}, u32[]{:S(2)}) copy-start(f32[256]{0:T(256)S(1)} %fusion.245) | copy-start | bytes 3076
  356.6 98.4 %all-gather.23.cloned.1.call-start = ((), (), s32[]{:S(2)}) async-start(), calls=%async_computation.21 | async-start | bytes 1622016 | tf_op jit(solution)/shard_map/all_gather | solution.py:168
  357.4 124.8 %all-gather.25.cloned.1.call-start = ((), (), s32[]{:S(2)}) async-start(), calls=%async_computation.22 | async-start | bytes 1622016 | tf_op jit(solution)/shard_map/all_gather | solution.py:169
  358.1 170.5 %all-gather.27.cloned.1.call-start = ((), (), s32[]{:S(2)}) async-start(), calls=%async_computation.24 | async-start | bytes 2621440 | tf_op jit(solution)/shard_map/all_gather | solution.py:237
  358.7 225.6 %reduce-scatter.31.cloned.1.call-start = ((), (), s32[]{:S(2)}) async-start(), calls=%async_computation.25 | async-start | bytes 2621440 | tf_op jit(solution)/shard_map/reduce_scatter | solution.py:246
  528.6 7.7 copy-start.153
  541.9 92.4 %all-gather.29.cloned.1.call-start = ((), (), s32[]{:S(2)}) async-start(), calls=%async_computation.26 | async-start | bytes 2621440 | tf_op jit(solution)/shard_map/all_gather | solution.py:251
  589.1 505.6 %reduce-scatter.49.cloned.1.call-start = ((), (), s32[]{:S(2)}) async-start(), calls=%async_computation.35 | async-start | bytes 1769472
  596.6 500.0 %reduce-scatter.51.cloned.1.call-start = ((), (), s32[]{:S(2)}) async-start(), calls=%async_computation.36 | async-start | bytes 1769472
  604.4 494.1 %reduce-scatter.53.cloned.1.call-start = ((), (), s32[]{:S(2)}) async-start(), calls=%async_computation.37 | async-start | bytes 1769472
  615.5 485.6 %reduce-scatter.45.cloned.1.call-start = ((), (), s32[]{:S(2)}) async-start(), calls=%async_computation.33 | async-start | bytes 294912
  657.6 291.4 %copy-start.15 = (f32[16,2,64,64]{3,2,1,0:T(8,128)S(1)}, f32[16,2,64,64]{3,2,1,0:T(8,128)}, u32[]{:S(2)}) copy-start(f32[16,2,64,64]{3,2,1,0:T(8,128)} %copy-done.14) | copy-start | bytes 1572868
  1022.5 79.9 %reduce-scatter.43.cloned.1.call-start = ((), (), s32[]{:S(2)}) async-start(), calls=%async_computation.32 | async-start | bytes 294912
  1025.5 103.6 %reduce-scatter.37.cloned.1.call-start = ((), (), s32[]{:S(2)}) async-start(), calls=%async_computation.29 | async-start | bytes 589824 | tf_op jit(solution)/shard_map/reduce_scatter | solution.py:269
  1038.0 128.3 %reduce-scatter.35.cloned.1.call-start = ((), (), s32[]{:S(2)}) async-start(), calls=%async_computation.28 | async-start | bytes 589824 | tf_op jit(solution)/shard_map/reduce_scatter | solution.py:266
  1043.7 161.7 %reduce-scatter.47.cloned.1.call-start = ((), (), s32[]{:S(2)}) async-start(), calls=%async_computation.34 | async-start | bytes 1179648
  1057.4 187.3 %reduce-scatter.39.cloned.1.call-start = ((), (), s32[]{:S(2)}) async-start(), calls=%async_computation.30 | async-start | bytes 1179648 | tf_op jit(solution)/shard_map/reduce_scatter | solution.py:272
  1069.1 214.8 %reduce-scatter.41.cloned.1.call-start = ((), (), s32[]{:S(2)}) async-start(), calls=%async_computation.31 | async-start | bytes 1179648 | tf_op jit(solution)/shard_map/reduce_scatter | solution.py:275
  1078.2 251.6 %reduce-scatter.33.cloned.1.call-start = ((), (), s32[]{:S(2)}) async-start(), calls=%async_computation.27 | async-start | bytes 2621440 | tf_op jit(solution)/shard_map/reduce_scatter | solution.py:260
  1088.7 286.1 %reduce-scatter.29.cloned.1.call-start = ((), (), s32[]{:S(2)}) async-start(), calls=%async_computation.23 | async-start | bytes 2621440 | tf_op jit(solution)/shard_map/reduce_scatter | solution.py:216
  1094.6 412.8 %all-reduce.31.cloned.1.call-start = ((), (), s32[]{:S(2)}) async-start(), calls=%async_computation.38 | async-start | bytes 151552 | tf_op jit(solution)/shard_map/psum | solution.py:297
  1095.8 234.0 %copy-start.29 = (bf16[256,1024]{1,0:T(8,128)(2,1)S(1)}, bf16[256,1024]{1,0:T(8,128)(2,1)}, u32[]{:S(2)}) copy-start(bf16[256,1024]{1,0:T(8,128)(2,1)} %param.24) | copy-start | bytes 1572868
  1095.8 234.0 %copy-start.104 = (f32[1024]{0:T(1024)S(1)}, f32[1024]{0:T(1024)}, u32[]{:S(2)}) copy-start(f32[1024]{0:T(1024)} %param.26) | copy-start | bytes 12292
  1095.8 234.0 %copy-start.120 = (f32[256]{0:T(256)S(1)}, f32[256]{0:T(256)}, u32[]{:S(2)}) copy-start(f32[256]{0:T(256)} %copy-done.119) | copy-start | bytes 3076
  1098.4 233.5 %copy-start.140 = (f32[256]{0:T(256)S(1)}, f32[256]{0:T(256)}, u32[]{:S(2)}) copy-start(f32[256]{0:T(256)} %copy-done.139) | copy-start | bytes 3076
  1098.4 276.4 %copy-start.19 = (f32[256,1024]{1,0:T(8,128)S(1)}, f32[256,1024]{1,0:T(8,128)}, u32[]{:S(2)}) copy-start(f32[256,1024]{1,0:T(8,128)} %copy-done.17) | copy-start | bytes 3145732
  1098.4 276.4 %copy-start.52 = (bf16[256,1024]{1,0:T(8,128)(2,1)S(1)}, bf16[256,1024]{1,0:T(8,128)(2,1)}, u32[]{:S(2)}) copy-start(bf16[256,1024]{1,0:T(8,128)(2,1)} %param.25) | copy-start | bytes 1572868
  1098.4 276.4 %copy-start.53 = (bf16[256,1024]{1,0:T(8,128)(2,1)S(1)}, bf16[256,1024]{1,0:T(8,128)(2,1)}, u32[]{:S(2)}) copy-start(bf16[256,1024]{1,0:T(8,128)(2,1)} %reduce-scatter.31.cloned.1.call-done) | copy-start | bytes 1572868
  1098.4 276.4 %copy-start.103 = (f32[1024]{0:T(1024)S(1)}, f32[1024]{0:T(1024)}, u32[]{:S(2)}) copy-start(f32[1024]{0:T(1024)} %param.27) | copy-start | bytes 12292
  1098.4 276.4 %copy-start.110 = (f32[256]{0:T(256)S(1)}, f32[256]{0:T(256)}, u32[]{:S(2)}) copy-start(f32[256]{0:T(256)} %copy-done.109) | copy-start | bytes 3076
  1098.4 276.4 %copy-start.122 = (f32[256]{0:T(256)S(1)}, f32[256]{0:T(256)}, u32[]{:S(2)}) copy-start(f32[256]{0:T(256)} %copy-done.121) | copy-start | bytes 3076
  1100.7 231.2 %copy-start.147 = (f32[8]{0:T(128)}, f32[8]{0:T(128)S(1)}, u32[]{:S(2)}) copy-start(f32[8]{0:T(128)S(1)} %dynamic_update_slice.84) | copy-start | bytes 100
  1100.7 231.2 %copy-start.101 = (f32[4,1024]{1,0:T(4,128)}, f32[4,1024]{1,0:T(4,128)S(1)}, u32[]{:S(2)}) copy-start(f32[4,1024]{1,0:T(4,128)S(1)} %add_dynamic-update-slice_fusion.1) | copy-start | bytes 49156
  1100.8 231.2 %copy-start.100 = (f32[4,1024]{1,0:T(4,128)}, f32[4,1024]{1,0:T(4,128)S(1)}, u32[]{:S(2)}) copy-start(f32[4,1024]{1,0:T(4,128)S(1)} %add_dynamic-update-slice_fusion.2) | copy-start | bytes 49156
  1100.8 231.1 %copy-start.95 = (f32[4,2048]{1,0:T(4,128)}, f32[4,2048]{1,0:T(4,128)S(1)}, u32[]{:S(2)}) copy-start(f32[4,2048]{1,0:T(4,128)S(1)} %add_dynamic-update-slice_fusion) | copy-start | bytes 98308
  1101.0 230.9 %copy-start.146 = (f32[8]{0:T(128)}, f32[8]{0:T(128)S(1)}, u32[]{:S(2)}) copy-start(f32[8]{0:T(128)S(1)} %multiply_dynamic-update-slice_fusion) | copy-start | bytes 100
  (152 other events, 484.9 us)
Sparse Core Ops, SparseCore 0:
  10.8 47.5 all-gather.10
  60.2 22.7 all-gather.12
  84.9 23.3 all-gather.14
  110.0 23.4 all-gather.16
  277.5 75.5 reduce-scatter.26
  354.8 26.4 all-gather.20
  383.4 45.0 all-gather.18
  430.4 24.5 all-gather.22
  456.9 25.1 all-gather.24
  483.5 45.0 all-gather.26
  542.0 42.1 reduce-scatter.30
  589.2 45.0 all-gather.28
  637.6 37.1 reduce-scatter.48
  677.9 38.4 reduce-scatter.50
  719.5 38.4 reduce-scatter.52
  1022.7 32.1 reduce-scatter.44
  1058.3 33.6 reduce-scatter.42
  1094.9 34.1 reduce-scatter.36
  1132.2 34.0 reduce-scatter.34
  1169.3 36.1 reduce-scatter.46
  1208.7 35.9 reduce-scatter.38
  1247.8 35.9 reduce-scatter.40
  1286.1 43.5 reduce-scatter.32
  1331.9 42.8 reduce-scatter.28
  1382.9 124.4 all-reduce.30
where the time goes:
time: 1540 us; the launch traced here: 1520 us
  waiting for transfers between devices  692 us (45%)
  matrix products  382 us (25%)
  local copies, waits for them, and re-layouts  255 us (17%)
  other arithmetic  136 us (9%)
  blocking collectives  39.5 us (3%)
  between operations  16.6 us (1%)
    psum x1, waiting for transfers between devices, local(): lax.psum((d_gain_attn, d_gain_ffn, place_cols(mixer_grads[6], conv_query....  130 us
    squeeze x96, local copies, waits for them, and re-layouts, delta_mixer(): lax.scan(jax.checkpoint(span_step), start_state, by_block)  98.1 us
    reduce_scatter x1, waiting for transfers between devices, local(): lax.psum_scatter(jnp.dot(mixed_low, gathered[6], preferred_element_type=j...  75.1 us
    dot_general x64, matrix products, span_step(): jnp.einsum('shcd,shde->shce', queries, carried, precision=PRECISE)  51.2 us
    dot_general x64, matrix products, span_step(): jnp.einsum('shcd,shde->shce', w_rows, carried, precision=PRECISE)  49.9 us
    dot_general x48, matrix products, span_step(): jnp.einsum('shij,shje->shie', inner_mix, new_values, precision=PRECISE)  47.9 us
    all_gather x1, waiting for transfers between devices, local(): lax.all_gather(normed_two.astype(jnp.bfloat16), 'tensor', axis=0, tiled=T...  47.2 us
    all_gather x1, waiting for transfers between devices, local(): cot_rows = lax.all_gather(cotangent, 'tensor', axis=0, tiled=True)  46.5 us
  transfers between devices with their start and end apart: 25, of which 17 were waited for; matrix products, arithmetic and copies ran while one was open for 47% of the time, Pallas kernels for 0%

commit v1 on v0

v1 whole, which is shorter than its diff:
```python
import functools
import jax
import jax.numpy as jnp
from jax import lax
from jax.experimental import pallas as pl
from jax.experimental.pallas import tpu as pltpu
from jax.sharding import PartitionSpec as P

DK = 128
DV = 256
CONV = 4
SPAN = 64
SEQ_LEN = 1024
LANES = 128
F32 = jnp.float32
LOW = jnp.bfloat16


def mm(left, right, dims=((1,), (0,))):
    return lax.dot_general(
        left.astype(LOW), right.astype(LOW), (dims, ((), ())), preferred_element_type=F32
    )


NT = ((1,), (1,))
TN = ((0,), (0,))


def exact_dot(ones_mat, values):
    first = values.astype(LOW)
    rest = values - first.astype(F32)
    second = rest.astype(LOW)
    third = (rest - second.astype(F32)).astype(LOW)
    return mm(ones_mat, third) + mm(ones_mat, second) + mm(ones_mat, first)


def sigmoid(values):
    return 1.0 / (1.0 + jnp.exp(-values))


def softplus(values):
    return jnp.maximum(values, 0.0) + jnp.log1p(jnp.exp(-jnp.abs(values)))


def block_ones(rows, upper):
    row_ids = lax.broadcasted_iota(jnp.int32, (rows, rows), 0)
    col_ids = lax.broadcasted_iota(jnp.int32, (rows, rows), 1)
    same = (row_ids // SPAN) == (col_ids // SPAN)
    side = (row_ids <= col_ids) if upper else (row_ids >= col_ids)
    return jnp.where(same & side, 1.0, 0.0).astype(LOW)


def span_ids():
    return (
        lax.broadcasted_iota(jnp.int32, (SPAN, SPAN), 0),
        lax.broadcasted_iota(jnp.int32, (SPAN, SPAN), 1),
    )


def unit_lower_inverses(lowers):
    row_ids, col_ids = span_ids()
    inverses = None
    size = 1
    while size < SPAN:
        joined = (row_ids // (2 * size) == col_ids // (2 * size)) & (
            (row_ids // size) % 2 == 1
        ) & ((col_ids // size) % 2 == 0)
        parts = [jnp.where(joined, lower, 0.0) for lower in lowers]
        if inverses is None:
            eye = jnp.where(row_ids == col_ids, 1.0, 0.0)
            inverses = [eye - part for part in parts]
        else:
            halves = [mm(inverse, part) for inverse, part in zip(inverses, parts)]
            inverses = [
                inverse - mm(half, inverse) for half, inverse in zip(halves, inverses)
            ]
        size *= 2
    return inverses


class Columns:
    def __init__(self, head_count):
        self.q = 0
        self.k = head_count * DK
        self.v = 2 * head_count * DK
        self.o = self.v + head_count * DV
        self.ab = self.o + head_count * DV
        self.width = self.ab + LANES


def gates(ab_rows, par_ref, rows, head_count):
    shifted = ab_rows + par_ref[0:1, :]
    log_decay = -jnp.exp(par_ref[1:2, :]) * softplus(shifted)
    lane = lax.broadcasted_iota(jnp.int32, (rows, LANES), 1)
    log_decay = jnp.where(lane < head_count, log_decay, 0.0)
    cumulative = exact_dot(block_ones(rows, False), log_decay)
    beta = sigmoid(ab_rows)
    return shifted, log_decay, cumulative, beta


def conv_rows(padded, taps, start, cols):
    first = 8 - (CONV - 1) + start
    total = padded[first : first + SPAN, cols] * taps[0:1, :]
    for offset in range(1, CONV):
        total = total + padded[first + offset : first + offset + SPAN, cols] * taps[
            offset : offset + 1, :
        ]
    return total


def pair_inputs(head, block, cols, padded, taps_q, taps_k, taps_v, scal):
    cumulative, cum_t, beta, grow, fade = scal
    start = block * SPAN
    rows = slice(start, start + SPAN)
    qs = slice(cols.q + head * DK, cols.q + (head + 1) * DK)
    ks = slice(cols.k + head * DK, cols.k + (head + 1) * DK)
    vs = slice(cols.v + head * DV, cols.v + (head + 1) * DV)
    hk = slice(head * DK, (head + 1) * DK)
    hv = slice(head * DV, (head + 1) * DV)
    sq = conv_rows(padded, taps_q[:, hk], start, qs)
    sk = conv_rows(padded, taps_k[:, hk], start, ks)
    sv = conv_rows(padded, taps_v[:, hv], start, vs)
    gq, gk, gv = sigmoid(sq), sigmoid(sk), sigmoid(sv)
    cq, ck, cv = sq * gq, sk * gk, sv * gv
    rq = lax.rsqrt(jnp.sum(cq * cq, -1, keepdims=True) + 1e-06)
    rk = lax.rsqrt(jnp.sum(ck * ck, -1, keepdims=True) + 1e-06)
    unit_q = cq * rq
    key = ck * rk
    query = unit_q * DK ** (-0.5)
    cum_col = cumulative[rows, head : head + 1]
    cum_row = cum_t[head : head + 1, rows]
    row_ids, col_ids = span_ids()
    causal = row_ids >= col_ids
    decays = jnp.where(causal, jnp.exp(jnp.where(causal, cum_col - cum_row, 0.0)), 0.0)
    beta_col = beta[rows, head_lane(head, taps_q) : head_lane(head, taps_q) + 1]
    grow_col = grow[rows, head : head + 1]
    fade_col = fade[rows, head : head + 1]
    return dict(
        sq=sq, sk=sk, sv=sv, gq=gq, gk=gk, gv=gv, rq=rq, rk=rk, unit_q=unit_q, key=key,
        query=query, value=cv, decays=decays, beta=beta_col, grow=grow_col, fade=fade_col,
        strict=row_ids > col_ids,
    )


def head_lane(head, taps_q):
    return taps_q.shape[1] // DK + head


def chunk_scalars(ab_rows, par_ref, rows, head_count):
    shifted, log_decay, cumulative, beta = gates(ab_rows, par_ref, rows, head_count)
    cum_t = cumulative.T
    grow = jnp.exp(cumulative)
    fades = []
    ends = []
    for block in range(rows // SPAN):
        last = cumulative[(block + 1) * SPAN - 1 : (block + 1) * SPAN, :]
        fades.append(jnp.exp(last - cumulative[block * SPAN : (block + 1) * SPAN, :]))
        ends.append(jnp.exp(last))
    fade = jnp.concatenate(fades, 0) if len(fades) > 1 else fades[0]
    return shifted, log_decay, (cumulative, cum_t, beta, grow, fade), ends


def forward_kernel(
    head_count, rows, rank_ref, pre_ref, tq_ref, tk_ref, tv_ref, par_ref, gain_ref,
    mixed_ref, core_ref, state_ref, newv_ref, inv_ref, wrow_ref, carried, padded,
):
    cols = Columns(head_count)
    blocks = rows // SPAN
    conv_width = cols.o

    @pl.when(pl.program_id(1) == 0)
    def _():
        carried[...] = jnp.zeros_like(carried)
        padded[0:8, :] = jnp.zeros((8, conv_width), F32)

    @pl.when(pl.program_id(1) > 0)
    def _():
        padded[0:8, :] = padded[rows : rows + 8, :]

    padded[8 : 8 + rows, :] = pre_ref[:, 0:conv_width]
    _, _, scal, ends = chunk_scalars(
        pre_ref[:, cols.ab : cols.ab + LANES], par_ref, rows, head_count
    )
    taps = (tq_ref[...], tk_ref[...], tv_ref[...])
    pairs = [(block, head) for block in range(blocks) for head in range(head_count)]
    inputs, inners, lowers = [], [], []
    for block, head in pairs:
        got = pair_inputs(head, block, cols, padded, *taps, scal)
        both = jnp.concatenate([got["query"].astype(LOW), got["key"].astype(LOW)], 0)
        products = mm(both, got["key"], NT)
        inners.append((products[0:SPAN] * got["decays"]).astype(LOW))
        lowers.append(
            jnp.where(got["strict"], products[SPAN:] * got["decays"] * got["beta"], 0.0)
        )
        scaled = jnp.concatenate(
            [
                (got["beta"] * got["grow"] * got["key"]).astype(LOW),
                (got["beta"] * got["value"]).astype(LOW),
            ],
            1,
        )
        inputs.append(
            (
                scaled,
                (got["grow"] * got["query"]).astype(LOW),
                (got["fade"] * got["key"]).astype(LOW),
            )
        )
    ready = {}
    for (block, head), inverse, (scaled, read, faded), inner in zip(
        pairs, unit_lower_inverses(lowers), inputs, inners
    ):
        span = slice(block * SPAN, (block + 1) * SPAN)
        inverse = inverse.astype(LOW)
        inv_ref[span, head * SPAN : (head + 1) * SPAN] = inverse
        solved = mm(inverse, scaled)
        w_rows = solved[:, 0:DK].astype(LOW)
        wrow_ref[span, head * DK : (head + 1) * DK] = w_rows
        ready[block, head] = (
            jnp.concatenate([read, w_rows], 0), solved[:, DK:], inner, faded
        )
    states = [carried[head] for head in range(head_count)]
    for block in range(blocks):
        for head in range(head_count):
            state = states[head]
            sides, u_rows, inner, faded = ready[block, head]
            span = slice(block * SPAN, (block + 1) * SPAN)
            hv = slice(head * DV, (head + 1) * DV)
            low_state = state.astype(LOW)
            state_ref[0, block, head] = low_state
            read = mm(sides, low_state)
            new_values = (u_rows - read[SPAN:]).astype(LOW)
            newv_ref[span, hv] = new_values
            states[head] = ends[block][0:1, head : head + 1] * state + mm(faded, new_values, TN)
            core = read[0:SPAN] + mm(inner, new_values)
            core_ref[span, hv] = core.astype(LOW)
            gate = pre_ref[span, cols.o + head * DV : cols.o + (head + 1) * DV]
            scale = lax.rsqrt(jnp.mean(core * core, -1, keepdims=True) + 1e-05)
            mixed_ref[span, hv] = (
                core * scale * gain_ref[...] * (gate * sigmoid(gate))
            ).astype(LOW)
    for head in range(head_count):
        carried[head] = states[head]


def mixer_forward(pre, taps_q, taps_k, taps_v, params, gain, rank, head_count, rows=256):
    cols = Columns(head_count)
    tokens = pre.shape[0]
    seqs = tokens // SEQ_LEN
    chunks = SEQ_LEN // rows
    blocks = rows // SPAN
    kw, vw = head_count * DK, head_count * DV
    at = lambda s, c, rk: (s * chunks + c, 0)
    spec = pltpu.PrefetchScalarGridSpec(
        num_scalar_prefetch=1,
        grid=(seqs, chunks),
        in_specs=[
            pl.BlockSpec((rows, cols.width), at),
            pl.BlockSpec((CONV, kw), lambda s, c, rk: (0, rk[0])),
            pl.BlockSpec((CONV, kw), lambda s, c, rk: (0, rk[0])),
            pl.BlockSpec((CONV, vw), lambda s, c, rk: (0, rk[0])),
            pl.BlockSpec((8, LANES), lambda s, c, rk: (0, 0)),
            pl.BlockSpec((1, DV), lambda s, c, rk: (0, 0)),
        ],
        out_specs=[
            pl.BlockSpec((rows, vw), at),
            pl.BlockSpec((rows, vw), at),
            pl.BlockSpec((1, blocks, head_count, DK, DV), lambda s, c, rk: (s, c, 0, 0, 0)),
            pl.BlockSpec((rows, vw), at),
            pl.BlockSpec((rows, head_count * SPAN), at),
            pl.BlockSpec((rows, kw), at),
        ],
        scratch_shapes=[
            pltpu.VMEM((head_count, DK, DV), F32),
            pltpu.VMEM((rows + 8, cols.o), F32),
        ],
    )
    shape = jax.ShapeDtypeStruct
    return pl.pallas_call(
        functools.partial(forward_kernel, head_count, rows),
        grid_spec=spec,
        out_shape=[
            shape((tokens, vw), LOW),
            shape((tokens, vw), LOW),
            shape((seqs, SEQ_LEN // SPAN, head_count, DK, DV), LOW),
            shape((tokens, vw), LOW),
            shape((tokens, head_count * SPAN), LOW),
            shape((tokens, kw), LOW),
        ],
        compiler_params=pltpu.CompilerParams(
            dimension_semantics=("arbitrary", "arbitrary"), vmem_limit_bytes=48 * 1024 * 1024
        ),
        name="mixer_forward",
    )(rank, pre, taps_q, taps_k, taps_v, params, gain)


def backward_kernel(
    head_count, rows, rank_ref, pre_ref, prev_ref, tq_ref, tk_ref, tv_ref, par_ref, gain_ref,
    dmix_ref, core_ref, state_ref, newv_ref, inv_ref, wrow_ref,
    dpre_ref, dtaps_ref, dpar_ref, dgain_ref, carried, padded, dconv,
):
    cols = Columns(head_count)
    blocks = rows // SPAN
    conv_width = cols.o
    chunk = pl.num_programs(1) - 1 - pl.program_id(1)

    @pl.when((pl.program_id(0) == 0) & (pl.program_id(1) == 0))
    def _():
        dtaps_ref[...] = jnp.zeros_like(dtaps_ref)
        dpar_ref[...] = jnp.zeros_like(dpar_ref)
        dgain_ref[...] = jnp.zeros_like(dgain_ref)

    @pl.when(pl.program_id(1) == 0)
    def _():
        carried[...] = jnp.zeros_like(carried)
        dconv[rows : rows + 8, :] = jnp.zeros((8, conv_width), F32)

    @pl.when(pl.program_id(1) > 0)
    def _():
        dconv[rows : rows + 8, :] = dconv[0:8, :]

    padded[0:8, :] = jnp.where(chunk > 0, prev_ref[:, 0:conv_width], 0.0)
    padded[8 : 8 + rows, :] = pre_ref[:, 0:conv_width]
    shifted, log_decay, scal, ends = chunk_scalars(
        pre_ref[:, cols.ab : cols.ab + LANES], par_ref, rows, head_count
    )
    beta_all = scal[2]
    taps = (tq_ref[...], tk_ref[...], tv_ref[...])
    row_ids, col_ids = span_ids()
    upper_ones = jnp.where(row_ids <= col_ids, 1.0, 0.0).astype(LOW)
    gain = gain_ref[...]
    dgain = jnp.zeros((1, DV), F32)
    ready = {}
    for block in range(blocks):
        span = slice(block * SPAN, (block + 1) * SPAN)
        for head in range(head_count):
            hv = slice(head * DV, (head + 1) * DV)
            got = pair_inputs(head, block, cols, padded, *taps, scal)
            gate = pre_ref[span, cols.o + head * DV : cols.o + (head + 1) * DV]
            core = core_ref[span, hv].astype(F32)
            d_mixed = dmix_ref[span, hv].astype(F32)
            scale = lax.rsqrt(jnp.mean(core * core, -1, keepdims=True) + 1e-05)
            unit = core * scale
            sig_gate = sigmoid(gate)
            act_gate = gate * sig_gate
            with_unit = d_mixed * unit
            dgain = dgain + jnp.sum(with_unit * act_gate, 0, keepdims=True)
            dpre_ref[span, cols.o + head * DV : cols.o + (head + 1) * DV] = (
                with_unit * gain * (sig_gate + act_gate * (1.0 - sig_gate))
            ).astype(LOW)
            d_unit = d_mixed * gain * act_gate
            d_core = (
                scale * (d_unit - unit * jnp.mean(d_unit * unit, -1, keepdims=True))
            ).astype(LOW)
            query, key = got["query"].astype(LOW), got["key"].astype(LOW)
            both = jnp.concatenate([query, key], 0)
            products = mm(both, key, NT)
            got["inner"] = products[0:SPAN] * got["decays"]
            got["kk"] = jnp.where(got["strict"], products[SPAN:] * got["decays"], 0.0)
            got["both"] = both
            got["read"] = got["grow"] * got["query"]
            got["faded"] = got["fade"] * got["key"]
            got["d_core"] = d_core
            got["from_read"] = mm(got["read"], d_core, TN)
            got["from_inner"] = mm(got["inner"], d_core, TN)
            ready[block, head] = got
    dgain_ref[...] += dgain
    d_states = [carried[head] for head in range(head_count)]
    for block in reversed(range(blocks)):
        for head in range(head_count):
            d_state = d_states[head]
            span = slice(block * SPAN, (block + 1) * SPAN)
            hv = slice(head * DV, (head + 1) * DV)
            got = ready[block, head]
            low_d = d_state.astype(LOW)
            d_new = (got["from_inner"] + mm(got["faded"], low_d)).astype(LOW)
            w_rows = wrow_ref[span, head * DK : (head + 1) * DK]
            end = ends[block][0:1, head : head + 1]
            got["d_faded"] = mm(newv_ref[span, hv], low_d, NT)
            kept = end * d_state
            got["d_end"] = jnp.sum(
                jnp.sum(kept * state_ref[0, block, head].astype(F32), 0, keepdims=True),
                1,
                keepdims=True,
            )
            d_states[head] = got["from_read"] - mm(w_rows, d_new, TN) + kept
            got["d_new"] = d_new
    for head in range(head_count):
        carried[head] = d_states[head]
    lane = lax.broadcasted_iota(jnp.int32, (SPAN, LANES), 1)
    d_cums, d_betas = [], []
    for block in range(blocks):
        span = slice(block * SPAN, (block + 1) * SPAN)
        summed = jnp.zeros((SPAN, LANES), F32)
        direct = jnp.zeros((SPAN, LANES), F32)
        d_beta_all = jnp.zeros((SPAN, LANES), F32)
        for head in range(head_count):
            got = ready[block, head]
            hv = slice(head * DV, (head + 1) * DV)
            inverse = inv_ref[span, head * SPAN : (head + 1) * SPAN]
            solved = mm(inverse, got["d_new"], TN)
            left = jnp.concatenate([got["d_core"], solved.astype(LOW)], 0)
            right = jnp.concatenate([state_ref[0, block, head], newv_ref[span, hv]], 0)
            wide = mm(left, right, NT)
            d_read, d_inner = wide[0:SPAN, 0:DK], wide[0:SPAN, DK:]
            d_wk = -wide[SPAN:, 0:DK]
            d_lower = jnp.where(got["strict"], -wide[SPAN:, DK:], 0.0)
            beta, grow, fade, key = got["beta"], got["grow"], got["fade"], got["key"]
            grown = grow * key
            with_grown = jnp.sum(d_wk * grown, -1, keepdims=True)
            lower_kk = d_lower * got["kk"]
            crossing = beta * lower_kk + d_inner * got["inner"]
            tails = jnp.where(got["strict"], mm(upper_ones, crossing), 0.0)
            faded_sum = jnp.sum(got["d_faded"] * got["faded"], -1, keepdims=True)
            point = (
                jnp.sum(d_read * got["read"], -1, keepdims=True)
                - faded_sum
                + beta * with_grown
            )
            whole = (
                jnp.sum(tails, -1, keepdims=True)
                + got["d_end"]
                + jnp.sum(faded_sum, 0, keepdims=True)
            )
            d_beta = (
                with_grown
                + jnp.sum(solved * got["value"], -1, keepdims=True)
                + jnp.sum(lower_kk, -1, keepdims=True)
            )
            summed = jnp.where(lane == head, point, summed)
            direct = jnp.where(lane == head, whole, direct)
            d_beta_all = jnp.where(lane == head_count + head, d_beta, d_beta_all)
            d_qk = d_inner * got["decays"]
            d_kk = d_lower * got["decays"] * beta
            d_both = jnp.concatenate([d_qk.astype(LOW), d_kk.astype(LOW)], 0)
            forward_part = mm(d_both, got["both"][SPAN:])
            d_query = grow * d_read + forward_part[0:SPAN]
            d_key = (
                fade * got["d_faded"]
                + beta * grow * d_wk
                + forward_part[SPAN:]
                + mm(d_both, got["both"], TN)
            )
            d_unit_q = d_query * DK ** (-0.5)
            unit_q = got["unit_q"]
            d_cq = got["rq"] * (
                d_unit_q - unit_q * jnp.sum(d_unit_q * unit_q, -1, keepdims=True)
            )
            d_ck = got["rk"] * (d_key - key * jnp.sum(d_key * key, -1, keepdims=True))
            d_cv = beta * solved
            for d_act, pre_act, sig, first, size in (
                (d_cq, got["sq"], got["gq"], cols.q + head * DK, DK),
                (d_ck, got["sk"], got["gk"], cols.k + head * DK, DK),
                (d_cv, got["sv"], got["gv"], cols.v + head * DV, DV),
            ):
                dconv[span, first : first + size] = d_act * sig * (1.0 + pre_act * (1.0 - sig))
        d_cums.append((summed, direct))
        d_betas.append(d_beta_all)
    join = lambda parts: jnp.concatenate(parts, 0) if len(parts) > 1 else parts[0]
    d_log = exact_dot(block_ones(rows, True), join([p[0] for p in d_cums])) + join(
        [p[1] for p in d_cums]
    )
    lanes_all = lax.broadcasted_iota(jnp.int32, (rows, LANES), 1)
    d_a = jnp.where(
        lanes_all < head_count, d_log * -jnp.exp(par_ref[1:2, :]) * sigmoid(shifted), 0.0
    )
    d_b = join(d_betas) * beta_all * (1.0 - beta_all)
    dpre_ref[:, cols.ab : cols.ab + LANES] = (d_a + d_b).astype(LOW)
    dpar_ref[0:1, :] += jnp.sum(d_a, 0, keepdims=True)
    dpar_ref[1:2, :] += jnp.sum(d_log * log_decay, 0, keepdims=True)
    for taps_now, base in ((taps[0], cols.q), (taps[1], cols.k), (taps[2], cols.v)):
        width = taps_now.shape[1]
        for part in range(width // LANES):
            col = slice(base + part * LANES, base + (part + 1) * LANES)
            for block in range(blocks):
                start = block * SPAN
                total = None
                now = dconv[start : start + SPAN, col]
                for tap in range(CONV):
                    ahead = start + CONV - 1 - tap
                    tap_row = taps_now[tap : tap + 1, part * LANES : (part + 1) * LANES]
                    term = (now if tap == CONV - 1 else dconv[ahead : ahead + SPAN, col]) * tap_row
                    total = term if total is None else total + term
                    behind = 8 - (CONV - 1) + tap + start
                    dtaps_ref[tap : tap + 1, col] += jnp.sum(
                        now * padded[behind : behind + SPAN, col], 0, keepdims=True
                    )
                dpre_ref[start : start + SPAN, col] = total.astype(LOW)


def mixer_backward(pre, taps_q, taps_k, taps_v, params, gain, rank, d_mixed, saved, head_count,
                   rows=256):
    cols = Columns(head_count)
    tokens = pre.shape[0]
    seqs = tokens // SEQ_LEN
    chunks = SEQ_LEN // rows
    blocks = rows // SPAN
    kw, vw = head_count * DK, head_count * DV
    at = lambda s, c, rk: (s * chunks + chunks - 1 - c, 0)
    before = lambda s, c, rk: (
        jnp.maximum((s * chunks + chunks - 1 - c) * (rows // 8) - 1, 0), 0)
    fixed = lambda s, c, rk: (0, 0)
    spec = pltpu.PrefetchScalarGridSpec(
        num_scalar_prefetch=1,
        grid=(seqs, chunks),
        in_specs=[
            pl.BlockSpec((rows, cols.width), at),
            pl.BlockSpec((8, cols.width), before),
            pl.BlockSpec((CONV, kw), lambda s, c, rk: (0, rk[0])),
            pl.BlockSpec((CONV, kw), lambda s, c, rk: (0, rk[0])),
            pl.BlockSpec((CONV, vw), lambda s, c, rk: (0, rk[0])),
            pl.BlockSpec((8, LANES), fixed),
            pl.BlockSpec((1, DV), fixed),
            pl.BlockSpec((rows, vw), at),
            pl.BlockSpec((rows, vw), at),
            pl.BlockSpec((1, blocks, head_count, DK, DV),
                         lambda s, c, rk: (s, chunks - 1 - c, 0, 0, 0)),
            pl.BlockSpec((rows, vw), at),
            pl.BlockSpec((rows, head_count * SPAN), at),
            pl.BlockSpec((rows, kw), at),
        ],
        out_specs=[
            pl.BlockSpec((rows, cols.width), at),
            pl.BlockSpec((CONV, cols.o), fixed),
            pl.BlockSpec((8, LANES), fixed),
            pl.BlockSpec((1, DV), fixed),
        ],
        scratch_shapes=[
            pltpu.VMEM((head_count, DK, DV), F32),
            pltpu.VMEM((rows + 8, cols.o), F32),
            pltpu.VMEM((rows + 8, cols.o), F32),
        ],
    )
    shape = jax.ShapeDtypeStruct
    return pl.pallas_call(
        functools.partial(backward_kernel, head_count, rows),
        grid_spec=spec,
        out_shape=[
            shape((tokens, cols.width), LOW),
            shape((CONV, cols.o), F32),
            shape((8, LANES), F32),
            shape((1, DV), F32),
        ],
        compiler_params=pltpu.CompilerParams(
            dimension_semantics=("arbitrary", "arbitrary"), vmem_limit_bytes=48 * 1024 * 1024
        ),
        name="mixer_backward",
    )(rank, pre, pre, taps_q, taps_k, taps_v, params, gain, d_mixed, *saved)


def rms_norm(values, gain):
    return values * lax.rsqrt(jnp.mean(values * values, -1, keepdims=True) + 1e-05) * gain


def swiglu_act(gate_val, up_val):
    return jax.nn.silu(gate_val) * up_val


def matmul_tn(left, right):
    return lax.dot_general(left, right, (TN, ((), ())), preferred_element_type=F32)


def matmul_nt(left, right):
    return lax.dot_general(left, right, (NT, ((), ())), preferred_element_type=F32)


def place_cols(member, width, offset):
    blank = jnp.zeros(member.shape[:-1] + (width,), F32)
    return lax.dynamic_update_slice_in_dim(blank, member, offset, member.ndim - 1)


def head_params(a_log, dt_bias, rank, head_count):
    slab = jnp.zeros((8, LANES), F32)
    bias = lax.dynamic_slice_in_dim(dt_bias, rank * head_count, head_count, 0)
    scale = lax.dynamic_slice_in_dim(a_log, rank * head_count, head_count, 0)
    slab = lax.dynamic_update_slice(slab, bias[None, :], (0, 0))
    return lax.dynamic_update_slice(slab, scale[None, :], (1, 0))


def join_mixer_weights(w_query, w_key, w_value, w_gate_out, w_decay, w_beta):
    blank = jnp.zeros((w_query.shape[0], LANES - 2 * w_decay.shape[1]), LOW)
    return jnp.concatenate(
        [w_query, w_key, w_value, w_gate_out, w_decay, w_beta, blank], axis=1
    )


def local_general(
    tokens, cotangent, gain_attn, gain_ffn, w_query, w_key, w_value, w_gate_out, w_decay,
    w_beta, w_output, w_ffn_gate, w_ffn_up, w_ffn_down, conv_query, conv_key, conv_value,
    a_log, dt_bias, out_gain,
):
    rank = lax.axis_index("tensor")
    head_count = w_decay.shape[1]
    cols = Columns(head_count)
    gather_rows = lambda value: lax.all_gather(value, "dp", axis=0, tiled=True)
    gather_cols = lambda value: lax.all_gather(value, "dp", axis=1, tiled=True)
    gather_tokens = lambda value: lax.all_gather(value, "tensor", axis=0, tiled=True)
    mixer_weights = gather_rows(
        join_mixer_weights(w_query, w_key, w_value, w_gate_out, w_decay, w_beta)
    )
    output_weights = gather_cols(w_output)
    gate_weights, up_weights = gather_rows(w_ffn_gate), gather_rows(w_ffn_up)
    down_weights = gather_cols(w_ffn_down)

    def scatter_tokens(value):
        return lax.psum_scatter(
            value.astype(LOW), "tensor", scatter_dimension=0, tiled=True
        ).astype(F32)

    tok_rows = tokens.astype(F32)
    normed_one, norm_one_pull = jax.vjp(rms_norm, tok_rows, gain_attn)
    mixer_in = gather_tokens(normed_one.astype(LOW))
    pre = jnp.dot(mixer_in, mixer_weights, preferred_element_type=F32)
    kernel_args = (
        pre, conv_query, conv_key, conv_value,
        head_params(a_log, dt_bias, rank, head_count), out_gain.reshape(1, DV),
        rank.reshape(1).astype(jnp.int32),
    )
    mixed, *saved = mixer_forward(*kernel_args, head_count)
    middle = tok_rows + scatter_tokens(
        jnp.dot(mixed, output_weights, preferred_element_type=F32)
    )
    normed_two, norm_two_pull = jax.vjp(rms_norm, middle, gain_ffn)
    ffn_in = gather_tokens(normed_two.astype(LOW))
    gate_val = jnp.dot(ffn_in, gate_weights, preferred_element_type=F32)
    up_val = jnp.dot(ffn_in, up_weights, preferred_element_type=F32)
    activated, swiglu_pull = jax.vjp(swiglu_act, gate_val, up_val)
    activated_low = activated.astype(LOW)
    output = (
        middle
        + scatter_tokens(jnp.dot(activated_low, down_weights, preferred_element_type=F32))
    ).astype(LOW)
    cot_rows = gather_tokens(cotangent)
    d_gate, d_up = swiglu_pull(matmul_nt(cot_rows, down_weights))
    d_gate, d_up = d_gate.astype(LOW), d_up.astype(LOW)
    grad_down = matmul_tn(activated_low, cot_rows)
    grad_gate, grad_up = matmul_tn(ffn_in, d_gate), matmul_tn(ffn_in, d_up)
    d_normed_two = scatter_tokens(
        matmul_nt(d_gate, gate_weights) + matmul_nt(d_up, up_weights)
    )
    d_middle_norm, d_gain_ffn = norm_two_pull(d_normed_two)
    d_middle = cotangent.astype(F32) + d_middle_norm
    branch_cot = gather_tokens(d_middle.astype(LOW))
    d_mixed = matmul_nt(branch_cot, output_weights).astype(LOW)
    grad_out = matmul_tn(mixed, branch_cot)
    d_pre, d_taps, d_heads, d_out_gain = mixer_backward(*kernel_args, d_mixed, saved, head_count)
    grad_mixer = matmul_tn(mixer_in, d_pre)
    d_normed_one = scatter_tokens(matmul_nt(d_pre, mixer_weights))
    d_tok_norm, d_gain_attn = norm_one_pull(d_normed_one)
    grad_tokens = d_middle + d_tok_norm

    def scatter_grad(value, dim):
        return lax.psum_scatter(
            value.astype(LOW), "dp", scatter_dimension=dim, tiled=True
        ).astype(F32)

    own_mixer = scatter_grad(grad_mixer, 0)
    edge = cols.ab + head_count
    small_sums = lax.psum(
        (
            d_gain_attn,
            d_gain_ffn,
            place_cols(d_taps[:, : cols.k], conv_query.shape[1], rank * cols.k),
            place_cols(d_taps[:, cols.k : cols.v], conv_key.shape[1], rank * cols.k),
            place_cols(d_taps[:, cols.v :], conv_value.shape[1], rank * (cols.o - cols.v)),
            place_cols(d_heads[1, :head_count], a_log.shape[0], rank * head_count),
            place_cols(d_heads[0, :head_count], dt_bias.shape[0], rank * head_count),
            d_out_gain[0],
        ),
        ("dp", "tensor"),
    )
    return (
        output, grad_tokens, small_sums[0], small_sums[1],
        own_mixer[:, : cols.k], own_mixer[:, cols.k : cols.v], own_mixer[:, cols.v : cols.o],
        own_mixer[:, cols.o : cols.ab], own_mixer[:, cols.ab : edge],
        own_mixer[:, edge : edge + head_count],
        scatter_grad(grad_out, 1), scatter_grad(grad_gate, 0), scatter_grad(grad_up, 0),
        scatter_grad(grad_down, 1), *small_sums[2:],
    )


def solution(mesh):
    spread = P(("dp", "tensor"), None)
    rows_split, cols_split = P("dp", "tensor"), P("tensor", "dp")
    return jax.shard_map(
        local_general,
        mesh=mesh,
        in_specs=(spread, spread, P(), P())
        + (rows_split,) * 6
        + (cols_split, rows_split, rows_split, cols_split)
        + (P(),) * 6,
        out_specs=(spread, spread, P(), P())
        + (rows_split,) * 6
        + (cols_split, rows_split, rows_split, cols_split)
        + (P(),) * 6,
        check_vma=False,
    )
```

time: 1540 us -> 915 us (0.59)
  matrix products: 382 us -> 79.3 us
  local copies, waits for them, and re-layouts: 255 us -> 35.2 us
  other arithmetic: 136 us -> 20.5 us
  Pallas kernels: 0 us -> 52.1 us
  blocking collectives: 39.5 us -> 0 us
    dot_general x296 -> x15, matrix products: 382 us -> 79.3 us  [the longest x5 26.4 us: matmul_tn(): lax.dot_general(left, right, (TN, ((), ())), preferred_element_type=F32)]
    reduce_scatter x8 -> x5, waiting for transfers between devices: 340 us -> 218 us  [the longest x4 172 us: scatter_tokens(): lax.psum_scatter(value.astype(LOW), 'tensor', scatter_dimension=0, tiled=...]
    squeeze x96 -> x0, local copies, waits for them, and re-layouts: 98.1 us -> none  [delta_mixer(): lax.scan(jax.checkpoint(span_step), start_state, by_block)]
    all_gather x10 -> x9, waiting for transfers between devices: 180 us -> 261 us  [the longest x4 162 us: local_general(): lax.all_gather(value, 'tensor', axis=0, tiled=True)]
    unnamed x31 -> x23, waiting for transfers between devices: 42.4 us -> 96.6 us
    pallas_call x0 -> x2, Pallas kernels: none -> 52.1 us  [the longest x1 33.2 us: mixer_backward(): pl.pallas_call(functools.partial(backward_kernel, head_count, rows), grid...]
    all_gather x4 -> x0, blocking collectives: 39.5 us -> none  [the longest x1 11.2 us: local(): lax.all_gather(w_key, 'dp', axis=0, tiled=True)]
    reduce_sum x41 -> x0, other arithmetic: 33.3 us -> none  [the longest x16 13.8 us: span_step(): weighted = key_rows * jnp.exp(final_log[..., None] - cumulative)[..., None]]
  transfers between devices with their start and end apart: 25 -> 19, of which waited for: 17 -> 17; matrix products, arithmetic and copies ran while one was open for 47% -> 11% of each run, Pallas kernels for 0% -> 6%
where the time goes in v1:
time: 915 us; the launch traced here: 906 us
  waiting for transfers between devices  703 us (77%)
  matrix products  79.3 us (9%)
  Pallas kernels  52.1 us (6%)
  local copies, waits for them, and re-layouts  35.2 us (4%)
  other arithmetic  20.5 us (2%)
  between operations  14.9 us (2%)
    reduce_scatter x4, waiting for transfers between devices, scatter_tokens(): lax.psum_scatter(value.astype(LOW), 'tensor', scatter_dimension=0, tiled=...  172 us
    all_gather x4, waiting for transfers between devices, local_general(): lax.all_gather(value, 'tensor', axis=0, tiled=True)  162 us
    psum x1, waiting for transfers between devices, local_general(): lax.psum((d_gain_attn, d_gain_ffn, place_cols(d_taps[:, :cols.k], conv_qu...  128 us
    unnamed x23, waiting for transfers between devices  96.6 us
    all_gather x3, waiting for transfers between devices, local_general(): gather_rows = lambda value: lax.all_gather(value, 'dp', axis=0, tiled=True)  77.1 us
    reduce_scatter x1, waiting for transfers between devices, scatter_grad(): lax.psum_scatter(value.astype(LOW), 'dp', scatter_dimension=dim, tiled=True)  46.9 us
    pallas_call x1, Pallas kernels, mixer_backward(): pl.pallas_call(functools.partial(backward_kernel, head_count, rows), grid...  33.2 us
    unnamed x90, local copies, waits for them, and re-layouts  29.5 us
  transfers between devices with their start and end apart: 19, of which 17 were waited for; matrix products, arithmetic and copies ran while one was open for 11% of the time, Pallas kernels for 6%

profile of v1, /device:TPU:1, one launch (start us, length us, event | category | flops | bytes accessed | tf_op | source)
XLA Modules:
  0.0 906.5 jit_solution(16602082294007301064)
XLA Ops:
  7.3 1.3 fusion.14
  8.7 2.0 fusion.8
  11.1 0.9 concatenate.3
  13.1 45.3 %all-gather.10.cloned.1.call-done = bf16[1024,1024]{1,0:T(8,128)(2,1)} async-done(((bf16[256,1024]{1,0:T(8,128)(2,1)}), bf16[1024,1024]{1,0:T(8,128)(2,1)}) %all-gather.10.cloned.1.call-update) | async-done | bytes 2097168 | tf_op jit(solution)/shard_map/all_gather | solution.py:597
  58.4 35.2 %all-gather.12.cloned.1.call-done = bf16[1024,1664]{1,0:T(8,128)(2,1)} async-done(((bf16[128,1664]{1,0:T(8,128)(2,1)}), bf16[1024,1664]{1,0:T(8,128)(2,1)}) %all-gather.12.cloned.1.call-update) | async-done | bytes 3407888 | tf_op jit(solution)/shard_map/all_gather | solution.py:595
  93.6 9.3 %fusion.22.pre_ref.prev_ref = f32[1024,1664]{1,0:T(8,128)} fusion(bf16[1024,1024]{1,0:T(8,128)(2,1)} %all-gather.10.cloned.1.call-done, bf16[1024,1664]{1,0:T(8,128)(2,1)} %all-gather.12.cloned.1.call-done), kind=kOutput, calls=%fused_computation.61 | convolution fusion | flops 3489660928 | bytes 12320768 | tf_op jit(solution)/shard_map/dot_general | solution.py:613
  102.9 19.0 %mixer_forward.1 = (bf16[1024,512]{1,0:T(8,128)(2,1)S(1)}, bf16[1024,512]{1,0:T(8,128)(2,1)S(1)}, bf16[1,16,2,128,256]{4,3,2,1,0:T(8,128)(2,1)S(1)}, bf16[1024,5...) custom-call(s32[1]{0:T(128)} %bitcast.rank_ref, ...), custom_call_target="tpu_custom_call" | custom-call | tf_op jit(solution)/shard_map/mixer_forward/pallas_call | solution.py:279
  121.9 1.0 copy-done.2
  122.9 1.0 copy-done.4
  124.7 4.2 convolution_convert_fusion.2
  129.5 42.3 %reduce-scatter.18.cloned.1.call-done = bf16[256,1024]{1,0:T(8,128)(2,1)} async-done(((bf16[1024,1024]{1,0:T(8,128)(2,1)}), bf16[256,1024]{1,0:T(8,128)(2,1)}) %reduce-scatter.18.cloned.1.call-update) | async-done | bytes 524304 | tf_op jit(solution)/shard_map/reduce_scatter | solution.py:606
  171.8 1.4 multiply_reduce_fusion
  173.3 2.2 multiply_convert_fusion.2
  178.0 20.8 %all-gather.18.cloned.1.call-done = bf16[1024,704]{0,1:T(8,128)(2,1)} async-done(((bf16[128,704]{0,1:T(8,128)(2,1)}), bf16[1024,704]{0,1:T(8,128)(2,1)}) %all-gather.18.cloned.1.call-update) | async-done | bytes 1441808 | tf_op jit(solution)/shard_map/all_gather | solution.py:595
  198.8 47.1 %all-gather.16.cloned.1.call-done = bf16[1024,1024]{1,0:T(8,128)(2,1)} async-done(((bf16[256,1024]{1,0:T(8,128)(2,1)}), bf16[1024,1024]{1,0:T(8,128)(2,1)}) %all-gather.16.cloned.1.call-update) | async-done | bytes 2097168 | tf_op jit(solution)/shard_map/all_gather | solution.py:597
  245.9 5.4 fusion.23
  251.3 21.1 %all-gather.20.cloned.1.call-done = bf16[1024,704]{0,1:T(8,128)(2,1)} async-done(((bf16[128,704]{0,1:T(8,128)(2,1)}), bf16[1024,704]{0,1:T(8,128)(2,1)}) %all-gather.20.cloned.1.call-update) | async-done | bytes 1441808 | tf_op jit(solution)/shard_map/all_gather | solution.py:595
  272.4 5.2 fusion.24
  277.6 21.9 %all-gather.22.cloned.1.call-done = bf16[704,1024]{1,0:T(8,128)(2,1)} async-done(((bf16[704,128]{1,0:T(8,128)(2,1)}), bf16[704,1024]{1,0:T(8,128)(2,1)}) %all-gather.22.cloned.1.call-update) | async-done | bytes 1441808 | tf_op jit(solution)/shard_map/all_gather | solution.py:596
  299.5 46.7 %all-gather.24.cloned.1.call-done = bf16[1024,1024]{1,0:T(8,128)(2,1)} async-done(((bf16[256,1024]{1,0:T(8,128)(2,1)}), bf16[1024,1024]{1,0:T(8,128)(2,1)}) %all-gather.24.cloned.1.call-update) | async-done | bytes 2097168 | tf_op jit(solution)/shard_map/all_gather | solution.py:597
  346.2 7.7 multiply_convert_fusion
  353.9 1.8 fusion.25
  356.3 3.3 add_convert_fusion
  359.7 42.3 %reduce-scatter.22.cloned.1.call-done = bf16[256,1024]{1,0:T(8,128)(2,1)} async-done(((bf16[1024,1024]{1,0:T(8,128)(2,1)}), bf16[256,1024]{1,0:T(8,128)(2,1)}) %reduce-scatter.22.cloned.1.call-update) | async-done | bytes 524304 | tf_op jit(solution)/shard_map/reduce_scatter | solution.py:606
  402.0 2.4 fusion.10
  404.4 2.7 fusion.18
  407.2 4.8 convolution_convert_fusion.5
  412.0 2.6 copy.50
  414.9 5.0 convolution_convert_fusion.4
  419.9 2.6 copy.52
  422.5 4.8 convolution_convert_fusion.6
  427.3 2.6 copy.54
  430.0 22.5 %all-gather.26.cloned.1.call-done = bf16[1024,1024]{1,0:T(8,128)(2,1)} async-done(((bf16[256,1024]{1,0:T(8,128)(2,1)}), bf16[1024,1024]{1,0:T(8,128)(2,1)}) %all-gather.26.cloned.1.call-update) | async-done | bytes 2097168 | tf_op jit(solution)/shard_map/all_gather | solution.py:597
  452.4 4.2 convolution_convert_fusion.7
  456.6 2.3 copy.48
  459.0 3.4 convolution_convert_fusion.8.dmix_ref
  462.4 33.2 %mixer_backward.1 = (bf16[1024,1664]{1,0:T(8,128)(2,1)}, f32[4,1024]{1,0:T(4,128)S(1)}, f32[8,128]{1,0:T(8,128)S(1)}, f32[1,256]{1,0:T(1,128)}) custom-call(s32[1]{0:T(128)} %bitcast.rank_ref, f32[1024,1664]{1,0:T(8,128)} %fusion.22.pre_ref.prev_ref, f32[1024,1664]{1,0:T(8,128)} %fusion.22.pre_ref.prev_ref, f32[4,1024]{1,0:T(4,128)S(1)} %copy-done.8, ...), custom_call_target="tpu_custom_call" | custom-call | tf_op jit(solution)/shard_map/mixer_backward/pallas_call | solution.py:535
  495.5 7.3 convolution_convert_fusion.1
  502.9 5.2 convolution_convert_fusion.3
  508.5 7.7 convolution_convert_fusion
  516.3 1.2 copy.51
  518.3 16.1 %reduce-scatter.32.cloned.1.call-done = bf16[128,704]{1,0:T(8,128)(2,1)} async-done(((bf16[1024,704]{1,0:T(8,128)(2,1)}), bf16[128,704]{1,0:T(8,128)(2,1)}) %reduce-scatter.32.cloned.1.call-update) | async-done | bytes 180240
  534.4 1.1 copy.53
  536.2 39.7 %reduce-scatter.34.cloned.1.call-done = bf16[128,704]{1,0:T(8,128)(2,1)} async-done(((bf16[1024,704]{1,0:T(8,128)(2,1)}), bf16[128,704]{1,0:T(8,128)(2,1)}) %reduce-scatter.34.cloned.1.call-update) | async-done | bytes 180240
  575.9 1.1 copy.55
  578.1 37.3 %reduce-scatter.28.cloned.1.call-done = bf16[128,512]{1,0:T(8,128)(2,1)} async-done(((bf16[1024,512]{1,0:T(8,128)(2,1)}), bf16[128,512]{1,0:T(8,128)(2,1)}) %reduce-scatter.28.cloned.1.call-update) | async-done | bytes 131088
  615.3 1.0 copy.49
  617.1 44.0 %reduce-scatter.24.cloned.1.call-done = bf16[256,1024]{1,0:T(8,128)(2,1)} async-done(((bf16[1024,1024]{1,0:T(8,128)(2,1)}), bf16[256,1024]{1,0:T(8,128)(2,1)}) %reduce-scatter.24.cloned.1.call-update) | async-done | bytes 524304 | tf_op jit(solution)/shard_map/reduce_scatter | solution.py:606
  661.1 2.1 fusion.11
  663.3 42.8 %reduce-scatter.20.cloned.1.call-done = bf16[256,1024]{1,0:T(8,128)(2,1)} async-done(((bf16[1024,1024]{1,0:T(8,128)(2,1)}), bf16[256,1024]{1,0:T(8,128)(2,1)}) %reduce-scatter.20.cloned.1.call-update) | async-done | bytes 524304 | tf_op jit(solution)/shard_map/reduce_scatter | solution.py:606
  706.2 3.1 fusion.13
  709.3 46.9 %reduce-scatter.26.cloned.1.call-done = bf16[128,1664]{1,0:T(8,128)(2,1)} async-done(((bf16[1024,1664]{1,0:T(8,128)(2,1)}), bf16[128,1664]{1,0:T(8,128)(2,1)}) %reduce-scatter.26.cloned.1.call-update) | async-done | bytes 426000 | tf_op jit(solution)/shard_map/reduce_scatter | solution.py:653
  756.2 1.8 fusion.20
  758.0 1.6 fusion.21
  759.6 0.9 fusion.19
  761.8 127.5 %all-reduce.4.cloned.1.call-done = (f32[1024]{0:T(1024)}, f32[1024]{0:T(1024)}, f32[4,1024]{1,0:T(4,128)}, f32[4,1024]{1,0:T(4,128)}, f32[4,2048]{1,0:T(4,128)}, /*index=5*/f32[8]{0:T(128)}, f32[8]{0:T(128)}, f32[256]{0:T(256)}) async-done(((f32[1024]{0:T(1024)}, f32[1024]{0:T(1024)}, f32[4,1024]{1,0:T(4,128)}, f32[4,1024]{1,0:T(4,128)}, f32[4,2048]{1,0:T(4,128)}, /*index=5*/f32[8]{0:T(128)}, f32[8]{0:T(128)}, ...) | async-done | bytes 74832 | tf_op jit(solution)/shard_map/psum | solution.py:659
  889.4 1.3 copy.71
  890.6 1.3 copy.72
  891.9 1.3 copy.73
  893.2 1.3 copy.74
  894.5 1.4 copy.75
  895.9 1.2 copy.76
  897.1 1.2 copy.77
  898.3 1.2 copy.78
  (135 shorter events, 11.6 us)
Async XLA Ops:
  7.2 5.6 copy-start
  7.2 3.6 copy-start.24
  7.2 3.7 copy-start.25
  7.2 3.8 copy-start.18
  7.2 3.8 copy-start.19
  7.2 3.8 copy-start.15
  7.3 3.8 copy-start.16
  7.3 5.6 copy-start.32
  7.3 51.2 %all-gather.10.cloned.1.call-start = ((), (), s32[]{:S(2)}) async-start(), calls=%async_computation.9 | async-start | bytes 2621440 | tf_op jit(solution)/shard_map/all_gather | solution.py:597
  10.7 82.9 %all-gather.12.cloned.1.call-start = ((), (), s32[]{:S(2)}) async-start(), calls=%async_computation.10 | async-start | bytes 3833856 | tf_op jit(solution)/shard_map/all_gather | solution.py:595
  12.0 112.7 %all-gather.14.cloned.1.call-start = ((), (), s32[]{:S(2)}) async-start(), calls=%async_computation.11 | async-start | bytes 1179648 | tf_op jit(solution)/shard_map/all_gather | solution.py:596
  12.7 159.1 %reduce-scatter.18.cloned.1.call-start = ((), (), s32[]{:S(2)}) async-start(), calls=%async_computation.12 | async-start | bytes 2621440 | tf_op jit(solution)/shard_map/reduce_scatter | solution.py:606
  13.1 89.8 %copy-start.7 = (f32[4,2048]{1,0:T(4,128)S(1)}, f32[4,2048]{1,0:T(4,128)}, u32[]{:S(2)}) copy-start(f32[4,2048]{1,0:T(4,128)} %tv_ref.3) | copy-start | bytes 98308
  13.1 89.8 %copy-start.8 = (f32[4,1024]{1,0:T(4,128)S(1)}, f32[4,1024]{1,0:T(4,128)}, u32[]{:S(2)}) copy-start(f32[4,1024]{1,0:T(4,128)} %tq_ref.3) | copy-start | bytes 49156
  13.1 89.8 %copy-start.9 = (f32[4,1024]{1,0:T(4,128)S(1)}, f32[4,1024]{1,0:T(4,128)}, u32[]{:S(2)}) copy-start(f32[4,1024]{1,0:T(4,128)} %tk_ref.3) | copy-start | bytes 49156
  13.1 89.8 %copy-start.10 = (f32[256]{0:T(256)S(1)}, f32[256]{0:T(256)}, u32[]{:S(2)}) copy-start(f32[256]{0:T(256)} %param.39) | copy-start | bytes 3076
  121.9 1.0 copy-start.2
  122.9 1.0 copy-start.4
  123.8 0.8 copy-start.5
  128.8 44.5 %copy-start.22 = (f32[1024]{0:T(1024)S(1)}, f32[1024]{0:T(1024)}, u32[]{:S(2)}) copy-start(f32[1024]{0:T(1024)} %param.23) | copy-start | bytes 12292
  128.9 69.9 %all-gather.18.cloned.1.call-start = ((), (), s32[]{:S(2)}) async-start(), calls=%async_computation.14 | async-start | bytes 1622016 | tf_op jit(solution)/shard_map/all_gather | solution.py:595
  129.4 116.5 %all-gather.16.cloned.1.call-start = ((), (), s32[]{:S(2)}) async-start(), calls=%async_computation.13 | async-start | bytes 2621440 | tf_op jit(solution)/shard_map/all_gather | solution.py:597
  175.5 96.9 %all-gather.20.cloned.1.call-start = ((), (), s32[]{:S(2)}) async-start(), calls=%async_computation.15 | async-start | bytes 1622016 | tf_op jit(solution)/shard_map/all_gather | solution.py:595
  176.3 123.2 %all-gather.22.cloned.1.call-start = ((), (), s32[]{:S(2)}) async-start(), calls=%async_computation.16 | async-start | bytes 1622016 | tf_op jit(solution)/shard_map/all_gather | solution.py:596
  177.0 169.2 %all-gather.24.cloned.1.call-start = ((), (), s32[]{:S(2)}) async-start(), calls=%async_computation.18 | async-start | bytes 2621440 | tf_op jit(solution)/shard_map/all_gather | solution.py:597
  177.8 224.3 %reduce-scatter.22.cloned.1.call-start = ((), (), s32[]{:S(2)}) async-start(), calls=%async_computation.19 | async-start | bytes 2621440 | tf_op jit(solution)/shard_map/reduce_scatter | solution.py:606
  346.2 7.7 copy-start.30
  353.9 1.9 copy-start.33
  353.9 1.9 copy-start.34
  353.9 2.4 copy-start.31
  359.7 92.8 %all-gather.26.cloned.1.call-start = ((), (), s32[]{:S(2)}) async-start(), calls=%async_computation.20 | async-start | bytes 2621440 | tf_op jit(solution)/shard_map/all_gather | solution.py:597
  407.2 109.1 %reduce-scatter.30.cloned.1.call-start = ((), (), s32[]{:S(2)}) async-start(), calls=%async_computation.24 | async-start | bytes 1769472
  414.6 119.8 %reduce-scatter.32.cloned.1.call-start = ((), (), s32[]{:S(2)}) async-start(), calls=%async_computation.25 | async-start | bytes 1769472
  422.5 153.4 %reduce-scatter.34.cloned.1.call-start = ((), (), s32[]{:S(2)}) async-start(), calls=%async_computation.26 | async-start | bytes 1769472
  429.9 185.4 %reduce-scatter.28.cloned.1.call-start = ((), (), s32[]{:S(2)}) async-start(), calls=%async_computation.23 | async-start | bytes 1179648
  458.9 202.2 %reduce-scatter.24.cloned.1.call-start = ((), (), s32[]{:S(2)}) async-start(), calls=%async_computation.21 | async-start | bytes 2621440 | tf_op jit(solution)/shard_map/reduce_scatter | solution.py:606
  459.0 3.4 copy-start.3
  459.0 3.4 copy-start.6
  462.4 33.2 %copy-start.28 = (bf16[1024,1664]{1,0:T(8,128)(2,1)S(1)}, bf16[1024,1664]{1,0:T(8,128)(2,1)}, u32[]{:S(2)}) copy-start(bf16[1024,1664]{1,0:T(8,128)(2,1)} %all-gather.12.cloned.1.call-done) | copy-start | bytes 10223620
  502.8 203.3 %reduce-scatter.20.cloned.1.call-start = ((), (), s32[]{:S(2)}) async-start(), calls=%async_computation.17 | async-start | bytes 2621440 | tf_op jit(solution)/shard_map/reduce_scatter | solution.py:606
  502.9 5.6 copy-start.29
  508.2 248.1 %reduce-scatter.26.cloned.1.call-start = ((), (), s32[]{:S(2)}) async-start(), calls=%async_computation.22 | async-start | bytes 3833856 | tf_op jit(solution)/shard_map/reduce_scatter | solution.py:653
  516.2 145.0 %copy-start.11 = (bf16[256,1024]{1,0:T(8,128)(2,1)S(1)}, bf16[256,1024]{1,0:T(8,128)(2,1)}, u32[]{:S(2)}) copy-start(bf16[256,1024]{1,0:T(8,128)(2,1)} %param.20) | copy-start | bytes 1572868
  516.2 145.0 %copy-start.23 = (f32[1024]{0:T(1024)S(1)}, f32[1024]{0:T(1024)}, u32[]{:S(2)}) copy-start(f32[1024]{0:T(1024)} %param.22) | copy-start | bytes 12292
  516.2 373.2 %all-reduce.4.cloned.1.call-start = ((), (), s32[]{:S(2)}) async-start(), calls=%async_computation.27 | async-start | bytes 151552 | tf_op jit(solution)/shard_map/psum | solution.py:659
  517.5 188.7 %copy-start.12 = (bf16[256,1024]{1,0:T(8,128)(2,1)S(1)}, bf16[256,1024]{1,0:T(8,128)(2,1)}, u32[]{:S(2)}) copy-start(bf16[256,1024]{1,0:T(8,128)(2,1)} %reduce-scatter.18.cloned.1.call-done) | copy-start | bytes 1572868
  517.5 188.7 %copy-start.13 = (bf16[256,1024]{1,0:T(8,128)(2,1)S(1)}, bf16[256,1024]{1,0:T(8,128)(2,1)}, u32[]{:S(2)}) copy-start(bf16[256,1024]{1,0:T(8,128)(2,1)} %param.21) | copy-start | bytes 1572868
  517.5 188.6 %copy-start.14 = (bf16[256,1024]{1,0:T(8,128)(2,1)S(1)}, bf16[256,1024]{1,0:T(8,128)(2,1)}, u32[]{:S(2)}) copy-start(bf16[256,1024]{1,0:T(8,128)(2,1)} %reduce-scatter.22.cloned.1.call-done) | copy-start | bytes 1572868
  577.9 85.4 %copy-start.27 = (f32[8]{0:T(128)}, f32[8]{0:T(128)S(1)}, u32[]{:S(2)}) copy-start(f32[8]{0:T(128)S(1)} %bitcast_dynamic-update-slice_fusion) | copy-start | bytes 100
  577.9 85.3 %copy-start.26 = (f32[8]{0:T(128)}, f32[8]{0:T(128)S(1)}, u32[]{:S(2)}) copy-start(f32[8]{0:T(128)S(1)} %bitcast_dynamic-update-slice_fusion.1) | copy-start | bytes 100
  578.0 85.3 %copy-start.21 = (f32[4,1024]{1,0:T(4,128)}, f32[4,1024]{1,0:T(4,128)S(1)}, u32[]{:S(2)}) copy-start(f32[4,1024]{1,0:T(4,128)S(1)} %slice_dynamic-update-slice_fusion.1) | copy-start | bytes 49156
  578.0 85.3 %copy-start.20 = (f32[4,1024]{1,0:T(4,128)}, f32[4,1024]{1,0:T(4,128)S(1)}, u32[]{:S(2)}) copy-start(f32[4,1024]{1,0:T(4,128)S(1)} %slice_dynamic-update-slice_fusion.2) | copy-start | bytes 49156
  578.1 85.2 %copy-start.17 = (f32[4,2048]{1,0:T(4,128)}, f32[4,2048]{1,0:T(4,128)S(1)}, u32[]{:S(2)}) copy-start(f32[4,2048]{1,0:T(4,128)S(1)} %slice_dynamic-update-slice_fusion) | copy-start | bytes 98308
  706.1 193.4 %copy-start.1 = (f32[8]{0:T(128)S(1)}, f32[8]{0:T(128)}, u32[]{:S(2)}) copy-start(f32[8]{0:T(128)} %param.38) | copy-start | bytes 100
Sparse Core Ops, SparseCore 0:
  10.8 47.5 all-gather.9
  60.9 32.6 all-gather.11
  95.5 23.4 all-gather.13
  129.0 42.8 reduce-scatter.17
  173.6 25.2 all-gather.17
  200.8 45.0 all-gather.15
  247.8 24.5 all-gather.19
  274.3 25.1 all-gather.21
  301.1 45.0 all-gather.23
  359.8 42.1 reduce-scatter.21
  407.3 45.0 all-gather.25
  455.6 37.0 reduce-scatter.29
  496.0 38.3 reduce-scatter.31
  537.5 38.3 reduce-scatter.33
  579.5 35.7 reduce-scatter.27
  617.5 43.5 reduce-scatter.23
  663.3 42.8 reduce-scatter.19
  709.4 46.7 reduce-scatter.25
  764.4 124.9 all-reduce.3

commit v2 on v1

--- a/solution.py
+++ b/solution.py
@@ -250,7 +250,7 @@
     chunks = SEQ_LEN // rows
     blocks = rows // SPAN
     kw, vw = head_count * DK, head_count * DV
-    at = lambda s, c, rk: (s * chunks + c, 0)
+    at = lambda s, c, rk: (s * chunks + (c ^ rk[1]), 0)
     spec = pltpu.PrefetchScalarGridSpec(
         num_scalar_prefetch=1,
         grid=(seqs, chunks),
@@ -496,9 +496,9 @@
     chunks = SEQ_LEN // rows
     blocks = rows // SPAN
     kw, vw = head_count * DK, head_count * DV
-    at = lambda s, c, rk: (s * chunks + chunks - 1 - c, 0)
+    at = lambda s, c, rk: (s * chunks + ((chunks - 1 - c) ^ rk[1]), 0)
     before = lambda s, c, rk: (
-        jnp.maximum((s * chunks + chunks - 1 - c) * (rows // 8) - 1, 0), 0)
+        (s * chunks + (jnp.maximum(chunks - 2 - c, 0) ^ rk[1]) + 1) * (rows // 8) - 1, 0)
     fixed = lambda s, c, rk: (0, 0)
     spec = pltpu.PrefetchScalarGridSpec(
         num_scalar_prefetch=1,
@@ -614,7 +614,7 @@
     kernel_args = (
         pre, conv_query, conv_key, conv_value,
         head_params(a_log, dt_bias, rank, head_count), out_gain.reshape(1, DV),
-        rank.reshape(1).astype(jnp.int32),
+        jnp.stack([rank, jnp.zeros_like(rank)]).astype(jnp.int32),
     )
     mixed, *saved = mixer_forward(*kernel_args, head_count)
     middle = tok_rows + scatter_tokens(
@@ -679,11 +679,199 @@
     )
 
 
+def local_paired(
+    tokens, cotangent, gain_attn, gain_ffn, w_query, w_key, w_value, w_gate_out, w_decay,
+    w_beta, w_output, w_ffn_gate, w_ffn_up, w_ffn_down, conv_query, conv_key, conv_value,
+    a_log, dt_bias, out_gain,
+):
+    n_tensor = 4
+    where_dp, z = lax.axis_index("dp"), lax.axis_index("tensor")
+    core, group = where_dp % 2, z // 2
+    home = core == group
+    own_quarter = z ^ (2 * (core ^ group))
+    rank = z ^ (2 * core)
+    head_count = w_decay.shape[1]
+    cols = Columns(head_count)
+    quarter, width = tokens.shape
+    chunk = width // 4
+
+    def send(value, move):
+        routes = []
+        for source in range(8):
+            for plane in range(n_tensor):
+                target = move(source, plane)
+                if target is not None:
+                    routes.append((source * n_tensor + plane, target[0] * n_tensor + target[1]))
+        return lax.ppermute(value, ("dp", "tensor"), routes)
+
+    by_core = lambda value: send(value, lambda d, p: (d ^ 1, p))
+    by_x = lambda value: send(value, lambda d, p: (d ^ 2, p))
+    by_y = lambda value: send(value, lambda d, p: (d ^ 4, p))
+    by_pair = lambda value: send(value, lambda d, p: (d, p ^ 1))
+    by_far = lambda value: send(value, lambda d, p: (d, p ^ 2))
+
+    def to_group(value, sent=None):
+        moved = send(
+            value.astype(sent or value.dtype),
+            lambda d, p: (d ^ 1, p ^ 2) if d % 2 != p // 2 else None,
+        )
+        return jnp.where(home, value, moved.astype(value.dtype))
+
+    x_odd, y_odd = (where_dp // 2) % 2 == 1, where_dp // 4 == 1
+
+    def reorder(value):
+        parts = [value[..., index * chunk : (index + 1) * chunk] for index in range(4)]
+        parts = [jnp.where(x_odd, parts[index ^ 1], parts[index]) for index in range(4)]
+        parts = [jnp.where(y_odd, parts[index ^ 2], parts[index]) for index in range(4)]
+        return jnp.concatenate(parts, -1)
+
+    def gather_group(value):
+        beside = by_pair(value)
+        across = by_core(value)
+        return jnp.concatenate([value, beside, across, by_core(beside)], 0)
+
+    def reduce_group(make):
+        far = make(slice(2 * quarter, 4 * quarter)).astype(LOW)
+        moved = by_core(far)
+        near = make(slice(0, 2 * quarter)) + moved.astype(F32)
+        beside = by_pair(near[quarter:].astype(LOW))
+        return near[:quarter] + beside.astype(F32)
+
+    def gather_weights(shard):
+        first = send(shard, lambda d, p: (d ^ 1, p) if d % 2 else (d ^ 1, p ^ 2))
+        second = send(shard, lambda d, p: (d, p ^ 2) if d % 2 else None)
+        held = jnp.concatenate(
+            [jnp.where(core == 0, shard, first), jnp.where(core == 0, first, second)], 0
+        )
+        half = shard.shape[0]
+        from_x, from_y = by_x(held), by_y(held)
+        diagonal = [by_x(from_y[:half]), by_y(from_x[half:])]
+        return [held, from_x, from_y, *diagonal]
+
+    def scatter_weights(grad):
+        grad = grad.astype(LOW)
+        half = grad.shape[0] // 8
+        part = lambda index: grad[2 * half * index : 2 * half * (index + 1)]
+        last = part(3)
+        from_x, from_y = by_x(last[:half]), by_y(last[half:])
+        add = lambda left, right: (left.astype(F32) + right.astype(F32)).astype(LOW)
+        to_y = jnp.concatenate([add(part(2)[:half], from_x), part(2)[half:]], 0)
+        to_x = jnp.concatenate([part(1)[:half], add(part(1)[half:], from_y)], 0)
+        total = (
+            part(0).astype(F32) + by_x(to_x).astype(F32) + by_y(to_y).astype(F32)
+        ).astype(LOW)
+        first = send(
+            jnp.where(core == 0, total[half:], total[:half]),
+            lambda d, p: (d ^ 1, p ^ 2) if d % 2 else (d ^ 1, p),
+        )
+        second = send(total[half:], lambda d, p: (d, p ^ 2) if d % 2 else None)
+        return first.astype(F32) + jnp.where(core == 0, total[:half], second).astype(F32)
+
+    def column_part(pieces, first, size):
+        return jnp.concatenate([piece[:, first : first + size] for piece in pieces], 0)
+
+    units = w_ffn_gate.shape[1]
+    mixer_pieces = gather_weights(
+        join_mixer_weights(w_query, w_key, w_value, w_gate_out, w_decay, w_beta)
+    )
+    mixer_weights = jnp.concatenate(mixer_pieces, 0)
+    down_end = -(-3 * units // LANES) * LANES
+    other_pieces = gather_weights(
+        jnp.concatenate(
+            [
+                w_ffn_gate, w_ffn_up, w_ffn_down.T,
+                jnp.zeros((w_ffn_gate.shape[0], down_end - 3 * units), LOW), w_output.T,
+            ],
+            1,
+        )
+    )
+    pair_weights = column_part(other_pieces, 0, 2 * units)
+    down_weights = column_part(other_pieces, 2 * units, units)
+    output_weights = column_part(other_pieces, down_end, w_output.shape[0])
+
+    gain_one, gain_two = reorder(gain_attn)[None, :], reorder(gain_ffn)[None, :]
+    tok_rows = reorder(to_group(tokens)).astype(F32)
+    cot_low = reorder(to_group(cotangent))
+    inverse_one = lax.rsqrt(jnp.mean(tok_rows * tok_rows, -1, keepdims=True) + 1e-05)
+    mixer_in = gather_group((tok_rows * inverse_one * gain_one).astype(LOW))
+    pre = jnp.dot(mixer_in, mixer_weights, preferred_element_type=F32)
+    kernel_args = (
+        pre, conv_query, conv_key, conv_value,
+        head_params(a_log, dt_bias, rank, head_count), out_gain.reshape(1, DV),
+        jnp.stack([rank, own_quarter]).astype(jnp.int32),
+    )
+    mixed, *saved = mixer_forward(*kernel_args, head_count, rows=quarter)
+    middle = tok_rows + reduce_group(lambda rows: matmul_nt(mixed[rows], output_weights))
+    inverse_two = lax.rsqrt(jnp.mean(middle * middle, -1, keepdims=True) + 1e-05)
+    ffn_in = gather_group((middle * inverse_two * gain_two).astype(LOW))
+    both_val = jnp.dot(ffn_in, pair_weights, preferred_element_type=F32)
+    gate_val, up_val = both_val[:, :units], both_val[:, units:]
+    gate_sig = jax.nn.sigmoid(gate_val)
+    gate_act = gate_val * gate_sig
+    activated = (gate_act * up_val).astype(LOW)
+    output = middle + reduce_group(lambda rows: matmul_nt(activated[rows], down_weights))
+    output = to_group(reorder(output.astype(LOW)))
+
+    cot_rows = gather_group(cot_low)
+    d_activated = jnp.dot(cot_rows, down_weights, preferred_element_type=F32)
+    d_gate = d_activated * up_val * gate_sig * (1.0 + gate_val * (1.0 - gate_sig))
+    d_both = jnp.concatenate([d_gate.astype(LOW), (d_activated * gate_act).astype(LOW)], 1)
+    d_two = reduce_group(lambda rows: matmul_nt(d_both[rows], pair_weights))
+    grad_pair = scatter_weights(matmul_tn(ffn_in, d_both))
+    grad_down = scatter_weights(matmul_tn(cot_rows, activated))
+
+    def norm_back(d_normed, values, inverse, gain):
+        scaled = d_normed * gain
+        unit = values * inverse
+        d_gain = jnp.sum(d_normed * unit, 0)
+        return d_gain, inverse * (scaled - unit * jnp.mean(scaled * unit, -1, keepdims=True))
+
+    d_gain_two, d_middle = norm_back(d_two, middle, inverse_two, gain_two)
+    d_middle = cot_low.astype(F32) + d_middle
+    branch_cot = gather_group(d_middle.astype(LOW))
+    d_mixed = jnp.dot(branch_cot, output_weights, preferred_element_type=F32).astype(LOW)
+    d_pre, d_taps, d_heads, d_out_gain = mixer_backward(
+        *kernel_args, d_mixed, saved, head_count, rows=quarter
+    )
+    grad_out = scatter_weights(matmul_tn(branch_cot, mixed))
+    grad_mixer = scatter_weights(matmul_tn(mixer_in, d_pre))
+    d_one = reduce_group(lambda rows: matmul_nt(d_pre[rows], mixer_weights))
+    d_gain_one, d_tokens = norm_back(d_one, tok_rows, inverse_one, gain_one)
+    grad_tokens = to_group(reorder(d_middle + d_tokens), LOW)
+
+    small = (
+        reorder(d_gain_one),
+        reorder(d_gain_two),
+        place_cols(d_taps[:, : cols.k], conv_query.shape[1], rank * cols.k),
+        place_cols(d_taps[:, cols.k : cols.v], conv_key.shape[1], rank * cols.k),
+        place_cols(d_taps[:, cols.v :], conv_value.shape[1], rank * (cols.o - cols.v)),
+        place_cols(d_heads[1, :head_count], a_log.shape[0], rank * head_count),
+        place_cols(d_heads[0, :head_count], dt_bias.shape[0], rank * head_count),
+        d_out_gain[0],
+    )
+    flat = jnp.concatenate([member.reshape(-1) for member in small])
+    for step in (by_core, by_x, by_y, by_pair, by_far):
+        flat = flat + step(flat)
+    sums, first = [], 0
+    for member in small:
+        sums.append(flat[first : first + member.size].reshape(member.shape))
+        first += member.size
+    edge = cols.ab + head_count
+    return (
+        output, grad_tokens, sums[0], sums[1],
+        grad_mixer[:, : cols.k], grad_mixer[:, cols.k : cols.v],
+        grad_mixer[:, cols.v : cols.o], grad_mixer[:, cols.o : cols.ab],
+        grad_mixer[:, cols.ab : edge], grad_mixer[:, edge : edge + head_count],
+        grad_out.T, grad_pair[:, :units], grad_pair[:, units:], grad_down.T, *sums[2:],
+    )
+
+
 def solution(mesh):
+    paired = mesh.shape["dp"] == 8 and mesh.shape["tensor"] == 4
     spread = P(("dp", "tensor"), None)
     rows_split, cols_split = P("dp", "tensor"), P("tensor", "dp")
     return jax.shard_map(
-        local_general,
+        local_paired if paired else local_general,
         mesh=mesh,
         in_specs=(spread, spread, P(), P())
         + (rows_split,) * 6

time: 915 us -> 474 us (0.52)
  waiting for transfers between devices: 703 us -> 222 us
  starting transfers between devices: 1.41 us -> 97.4 us
  matrix products: 79.3 us -> 52.1 us
  local copies, waits for them, and re-layouts: 35.2 us -> 22.1 us
  between operations: 14.9 us -> 2.61 us
    all_gather x9 -> x0, waiting for transfers between devices: 261 us -> none  [the longest x4 162 us: local_general(): lax.all_gather(value, 'tensor', axis=0, tiled=True)]
    ppermute x0 -> x65, waiting for transfers between devices: none -> 222 us  [send(): return lax.ppermute(value, ('dp', 'tensor'), routes)]
    reduce_scatter x5 -> x0, waiting for transfers between devices: 218 us -> none  [the longest x4 172 us: scatter_tokens(): lax.psum_scatter(value.astype(LOW), 'tensor', scatter_dimension=0, tiled=...]
    psum x1 -> x0, waiting for transfers between devices: 128 us -> none  [local_general(): lax.psum((d_gain_attn, d_gain_ffn, place_cols(d_taps[:, :cols.k], conv_qu...]
    ppermute x0 -> x65, starting transfers between devices: none -> 97.4 us  [send(): return lax.ppermute(value, ('dp', 'tensor'), routes)]
    unnamed x23 -> x0, waiting for transfers between devices: 96.6 us -> none
    unnamed x90 -> x124, local copies, waits for them, and re-layouts: 29.5 us -> 12 us
    dot_general x5 -> x4, matrix products: 26.4 us -> 14.1 us  [matmul_tn(): lax.dot_general(left, right, (TN, ((), ())), preferred_element_type=F32)]
  transfers between devices with their start and end apart: 19 -> 65, of which waited for: 17 -> 28; matrix products, arithmetic and copies ran while one was open for 11% -> 16% of each run, Pallas kernels for 6% -> 11%
where the time goes in v2:
time: 474 us; the launch traced here: 469 us
  waiting for transfers between devices  222 us (47%)
  starting transfers between devices  97.4 us (21%)
  Pallas kernels  53.4 us (11%)
  matrix products  52.1 us (11%)
  local copies, waits for them, and re-layouts  22.1 us (5%)
  other arithmetic  20.2 us (4%)
    ppermute x65, waiting for transfers between devices, send(): return lax.ppermute(value, ('dp', 'tensor'), routes)  222 us
    ppermute x65, starting transfers between devices, send(): return lax.ppermute(value, ('dp', 'tensor'), routes)  97.4 us
    pallas_call x1, Pallas kernels, mixer_backward(): pl.pallas_call(functools.partial(backward_kernel, head_count, rows), grid...  33.9 us
    pallas_call x1, Pallas kernels, mixer_forward(): pl.pallas_call(functools.partial(forward_kernel, head_count, rows), grid_...  19.4 us
    dot_general x8, matrix products, matmul_nt(): lax.dot_general(left, right, (NT, ((), ())), preferred_element_type=F32)  16.5 us
    dot_general x4, matrix products, matmul_tn(): lax.dot_general(left, right, (TN, ((), ())), preferred_element_type=F32)  14.1 us
    unnamed x124, local copies, waits for them, and re-layouts  12 us
  transfers between devices with their start and end apart: 65, of which 28 were waited for; matrix products, arithmetic and copies ran while one was open for 16% of the time, Pallas kernels for 11%

profile of v2, /device:TPU:1, one launch (start us, length us, event | category | flops | bytes accessed | tf_op | source)
XLA Modules:
  0.0 469.4 jit_solution(1992242657757485038)
XLA Ops:
  3.6 5.7 %collective-permute-start.5 = (bf16[128,1664]{1,0:T(8,128)(2,1)S(1)}, bf16[128,1664]{1,0:T(8,128)(2,1)}, u32[]{:S(2)}, u32[]{:S(2)}) collective-permute-start(bf16[128,1664]{1,0:T(8,128)(2,1)S(1)} %concatenate.88), channel_id=1, source_target_pairs={{4,6},{5,7},{6,4},{7,5},{12,14},{13,15},{14,12},{15,13},{20,22},{2... | collective-permute-start | bytes 1277960 | tf_op jit(solution)/shard_map/ppermute | solution.py:705
  12.2 1.9 collective-permute-start.11
  14.2 3.3 collective-permute-start
  18.0 33.6 %collective-permute-done.4 = bf16[128,1664]{1,0:T(8,128)(2,1)S(1)} collective-permute-done((bf16[128,1664]{1,0:T(8,128)(2,1)S(1)}, bf16[128,1664]{1,0:T(8,128)(2,1)S(1)}, u32[]{:S(2)}, u32[]{:S(2)}) %collective-permute-start.4) | collective-permute-done | bytes 426016 | tf_op jit(solution)/shard_map/ppermute | solution.py:705
  51.6 1.9 collective-permute-start.24
  56.6 16.8 %collective-permute-done = bf16[256,1024]{1,0:T(8,128)(2,1)} collective-permute-done((bf16[256,1024]{1,0:T(8,128)(2,1)}, bf16[256,1024]{1,0:T(8,128)(2,1)}, u32[]{:S(2)}, u32[]{:S(2)}) %collective-permute-start) | collective-permute-done | bytes 524320 | tf_op jit(solution)/shard_map/ppermute | solution.py:705
  74.6 4.3 collective-permute-done.24
  82.6 2.7 collective-permute-done.7
  86.7 3.6 collective-permute-done.1
  91.6 5.6 %collective-permute-done.8 = bf16[128,1664]{1,0:T(8,128)(2,1)S(1)} collective-permute-done((bf16[128,1664]{1,0:T(8,128)(2,1)S(1)}, bf16[128,1664]{1,0:T(8,128)(2,1)S(1)}, u32[]{:S(2)}, u32[]{:S(2)}) %collective-permute-start.8) | collective-permute-done | bytes 426016 | tf_op jit(solution)/shard_map/ppermute | solution.py:705
  98.6 25.2 %collective-permute-done.9 = bf16[128,1664]{1,0:T(8,128)(2,1)S(1)} collective-permute-done((bf16[128,1664]{1,0:T(8,128)(2,1)S(1)}, bf16[128,1664]{1,0:T(8,128)(2,1)S(1)}, u32[]{:S(2)}, u32[]{:S(2)}) %collective-permute-start.9) | collective-permute-done | bytes 426016 | tf_op jit(solution)/shard_map/ppermute | solution.py:705
  126.4 7.9 %fusion.37.pre_ref.prev_ref = f32[1024,1664]{1,0:T(8,128)} fusion(bf16[1024,1664]{1,0:T(8,128)(2,1)S(1)} %constant_dynamic-update-slice_fusion, bf16[256,1024]{1,0:T(8,128)(2,1)S(1)} %collective-permute-done.3, bf16[256,1024]{1,0:T(8,128)(2,1)S(1)} %collective-permute-done.2, bf16[256,1024]{1,0:T(8,128)(2,1)S(1)} %collective-permute-done.1, ...), kind=kOutput, calls=%fused_computation.119 | convolution fusion | flops 3498049536 | bytes 12320768 | tf_op jit(solution)/shard_map/dot_general | solution.py:797
  134.3 19.4 %mixer_forward.1 = (bf16[1024,512]{1,0:T(8,128)(2,1)S(1)}, bf16[1024,512]{1,0:T(8,128)(2,1)S(1)}, bf16[1,16,2,128,256]{4,3,2,1,0:T(8,128)(2,1)S(1)}, bf16[1024,5...) custom-call(s32[2]{0:T(128)S(1)} %pad_add_fusion.rank_ref, ...), custom_call_target="tpu_custom_call" | custom-call | tf_op jit(solution)/shard_map/mixer_forward/pallas_call | solution.py:279
  155.3 15.3 %collective-permute-done.15 = bf16[128,2688]{0,1:T(8,128)(2,1)S(1)} collective-permute-done((bf16[128,2688]{0,1:T(8,128)(2,1)S(1)}, bf16[128,2688]{0,1:T(8,128)(2,1)S(1)}, u32[]{:S(2)}, u32[]{:S(2)}) %collective-permute-start.15) | collective-permute-done | bytes 688160 | tf_op jit(solution)/shard_map/ppermute | solution.py:705
  173.1 1.9 collective-permute-done.16
  176.9 12.0 %collective-permute-done.17 = bf16[256,1024]{1,0:T(8,128)(2,1)S(1)} collective-permute-done((bf16[256,1024]{1,0:T(8,128)(2,1)S(1)}, bf16[256,1024]{1,0:T(8,128)(2,1)S(1)}, u32[]{:S(2)}, u32[]{:S(2)}) %collective-permute-start.17) | collective-permute-done | bytes 524320 | tf_op jit(solution)/shard_map/ppermute | solution.py:705
  190.6 1.6 collective-permute-start.19
  192.2 9.6 %collective-permute-done.18 = bf16[256,1024]{1,0:T(8,128)(2,1)S(1)} collective-permute-done((bf16[256,1024]{1,0:T(8,128)(2,1)S(1)}, bf16[256,1024]{1,0:T(8,128)(2,1)S(1)}, u32[]{:S(2)}, u32[]{:S(2)}) %collective-permute-start.18) | collective-permute-done | bytes 524320 | tf_op jit(solution)/shard_map/ppermute | solution.py:705
  201.7 2.1 collective-permute-start.20
  205.3 3.5 fusion.36
  208.8 7.3 %multiply_convert_fusion = (bf16[1024,704]{1,0:T(8,128)(2,1)S(1)}, bf16[1024,704]{1,0:T(8,128)(2,1)S(1)}, bf16[1024,704]{1,0:T(8,128)(2,1)S(1)}) fusion(f32[1024,1408]{1,0:T(8,128)S(1)} %fusion.36, bf16[1024,704]{0,1:T(8,128)(2,1)S(1)} %slice_dynamic-update-slice_fusion.8, bf16[256,1024]{1,0:T(8,128)(2,1)S(1)} %collective-permute-done.27, ...), kind=kOutput, calls=%fused_computation.7 | convolution fusion | flops 1501888512 | bytes 13631488 | tf_op jit(solution)/shard_map/dot_general | solution.py:816
  216.2 2.9 convolution_convert_fusion.2
  220.8 1.8 convolution_convert_fusion.5
  222.6 3.6 convolution_convert_fusion.1
  228.8 1.6 collective-permute-start.21
  230.9 4.5 collective-permute-done.53
  237.2 5.8 %collective-permute-done.60 = bf16[256,704]{0,1:T(8,128)(2,1)S(1)} collective-permute-done((bf16[256,704]{0,1:T(8,128)(2,1)S(1)}, bf16[256,704]{0,1:T(8,128)(2,1)S(1)}, u32[]{:S(2)}, u32[]{:S(2)}) %collective-permute-start.60) | collective-permute-done | bytes 360480 | tf_op jit(solution)/shard_map/ppermute | solution.py:705
  243.8 7.1 %collective-permute-start.63 = (bf16[128,704]{0,1:T(8,128)(2,1)S(1)}, bf16[128,704]{0,1:T(8,128)(2,1)S(1)}, u32[]{:S(2)}, u32[]{:S(2)}) collective-permute-start(bf16[128,704]{0,1:T(8,128)(2,1)S(1)} %get-tuple-element.131), channel_id=1, source_target_pairs={{0,4},{1,5},{2,6},{3,7},{4,2},{5,3},{6,0},{7,1},{8,12},{9,13},{10,... | collective-permute-start | bytes 540680 | tf_op jit(solution)/shard_map/ppermute | solution.py:705
  250.9 2.4 collective-permute-start.64
  254.7 5.2 %collective-permute-done.64 = bf16[128,704]{0,1:T(8,128)(2,1)S(1)} collective-permute-done((bf16[128,704]{0,1:T(8,128)(2,1)S(1)}, bf16[128,704]{0,1:T(8,128)(2,1)S(1)}, u32[]{:S(2)}, u32[]{:S(2)}) %collective-permute-start.64) | collective-permute-done | bytes 180256 | tf_op jit(solution)/shard_map/ppermute | solution.py:705
  261.8 1.8 convert_add_fusion.1
  263.7 1.5 collective-permute-start.29
  265.3 4.4 collective-permute-done.56
  270.1 4.5 collective-permute-start.57
  274.6 1.9 collective-permute-start.58
  276.5 14.8 %collective-permute-done.29 = bf16[256,1024]{1,0:T(8,128)(2,1)S(1)} collective-permute-done((bf16[256,1024]{1,0:T(8,128)(2,1)S(1)}, bf16[256,1024]{1,0:T(8,128)(2,1)S(1)}, u32[]{:S(2)}, u32[]{:S(2)}) %collective-permute-start.29) | collective-permute-done | bytes 524320 | tf_op jit(solution)/shard_map/ppermute | solution.py:705
  291.8 1.7 fusion.49
  294.5 8.1 %collective-permute-start.23 = (bf16[256,1024]{1,0:T(8,128)(2,1)}, bf16[256,1024]{1,0:T(8,128)(2,1)}, u32[]{:S(2)}, u32[]{:S(2)}) collective-permute-start(bf16[256,1024]{1,0:T(8,128)(2,1)} %pad_maximum_fusion.14), channel_id=1, source_target_pairs={{2,4},{3,5},{4,2},{5,3},{10,12},{11,13},{12,10},{13,11},{18,20},{1... | collective-permute-start | bytes 1572872 | tf_op jit(solution)/shard_map/ppermute | solution.py:705
  302.8 8.2 %collective-permute-done.30 = bf16[256,1024]{1,0:T(8,128)(2,1)} collective-permute-done((bf16[256,1024]{1,0:T(8,128)(2,1)}, bf16[256,1024]{1,0:T(8,128)(2,1)}, u32[]{:S(2)}, u32[]{:S(2)}) %collective-permute-start.30) | collective-permute-done | bytes 524320 | tf_op jit(solution)/shard_map/ppermute | solution.py:705
  312.1 1.9 copy.47
  314.0 1.9 copy.48
  316.5 2.1 broadcast_select_fusion.3
  318.6 3.2 convolution_convert_fusion.3
  323.2 2.8 convolution_convert_fusion.4.dmix_ref
  326.0 33.9 %mixer_backward.1 = (bf16[1024,1664]{1,0:T(8,128)(2,1)}, f32[4,1024]{1,0:T(4,128)S(1)}, f32[8,128]{1,0:T(8,128)S(1)}, f32[1,256]{1,0:T(1,128)S(1)}) custom-call(s32[2]{0:T(128)S(1)} %pad_add_fusion.rank_ref, f32[1024,1664]{1,0:T(8,128)} %fusion.37.pre_ref.prev_ref, f32[1024,1664]{1,0:T(8,128)} %fusion.37.pre_ref.prev_ref, f32[4,1024]{1,0:T(4,128)S(1)} %copy-done.8, ...), custom_call_target="tpu_custom_call" | custom-call | tf_op jit(solution)/shard_map/mixer_backward/pallas_call | solution.py:535
  360.0 4.7 fusion.11
  364.7 4.4 convolution_convert_fusion
  369.2 1.4 collective-permute-start.41
  371.1 1.5 collective-permute-start.33
  374.2 12.1 %collective-permute-done.48 = bf16[256,512]{1,0:T(8,128)(2,1)S(1)} collective-permute-done((bf16[256,512]{1,0:T(8,128)(2,1)S(1)}, bf16[256,512]{1,0:T(8,128)(2,1)S(1)}, u32[]{:S(2)}, u32[]{:S(2)}) %collective-permute-start.48) | collective-permute-done | bytes 262176 | tf_op jit(solution)/shard_map/ppermute | solution.py:705
  386.4 7.7 %collective-permute-start.51 = (bf16[128,512]{1,0:T(8,128)(2,1)S(1)}, bf16[128,512]{1,0:T(8,128)(2,1)S(1)}, u32[]{:S(2)}, u32[]{:S(2)}) collective-permute-start(bf16[128,512]{1,0:T(8,128)(2,1)S(1)} %get-tuple-element.133), channel_id=1, source_target_pairs={{0,4},{1,5},{2,6},{3,7},{4,2},{5,3},{6,0},{7,1},{8,12},{9,13},{10,... | collective-permute-start | bytes 393224 | tf_op jit(solution)/shard_map/ppermute | solution.py:705
  394.2 1.9 collective-permute-start.52
  399.1 1.6 collective-permute-done.52
  401.6 4.8 %convert_add_fusion = f32[512,1024]{1,0:T(8,128)S(1)} fusion(bf16[512,1024]{1,0:T(8,128)(2,1)} %collective-permute-done.33, bf16[1024,1664]{1,0:T(8,128)(2,1)} %copy-done.33, bf16[1024,1664]{1,0:T(8,128)(2,1)} %get-tuple-element.36), kind=kOutput, calls=%fused_computation.16 | convolution fusion | flops 1745879040 | bytes 8257536 | tf_op jit(solution)/shard_map/dot_general | solution.py:564
  406.6 2.2 collective-permute-start.34
  408.8 2.3 collective-permute-done.42
  411.9 2.0 add_convert_fusion
  414.9 3.2 collective-permute-start.45
  418.1 4.2 collective-permute-start.46
  423.8 1.6 fusion.22
  425.6 2.3 collective-permute-start.35
  429.2 22.0 %collective-permute-done.46 = bf16[128,1664]{1,0:T(8,128)(2,1)} collective-permute-done((bf16[128,1664]{1,0:T(8,128)(2,1)}, bf16[128,1664]{1,0:T(8,128)(2,1)}, u32[]{:S(2)}, u32[]{:S(2)}) %collective-permute-start.46) | collective-permute-done | bytes 426016 | tf_op jit(solution)/shard_map/ppermute | solution.py:705
  456.7 3.4 collective-permute-done.39
  461.5 2.9 collective-permute-done.40
  (320 shorter events, 67.8 us)
Async XLA Ops:
  3.5 48.1 %collective-permute-start.4 = (bf16[128,1664]{1,0:T(8,128)(2,1)S(1)}, bf16[128,1664]{1,0:T(8,128)(2,1)S(1)}, u32[]{:S(2)}, u32[]{:S(2)}) collective-permute-start(bf16[128,1664]{1,0:T(8,128)(2,1)S(1)} %concatenate.88), channel_id=1, source_target_pairs={{0,6},{1,7},{2,4},{3,5},{4,0},{5,1},{6,2},{7,3},{8,14},{9,15},{10,... | collective-permute-start | bytes 1277960 | tf_op jit(solution)/shard_map/ppermute | solution.py:705
  3.6 50.4 %collective-permute-start.5 = (bf16[128,1664]{1,0:T(8,128)(2,1)S(1)}, bf16[128,1664]{1,0:T(8,128)(2,1)}, u32[]{:S(2)}, u32[]{:S(2)}) collective-permute-start(bf16[128,1664]{1,0:T(8,128)(2,1)S(1)} %concatenate.88), channel_id=1, source_target_pairs={{4,6},{5,7},{6,4},{7,5},{12,14},{13,15},{14,12},{15,13},{20,22},{2... | collective-permute-start | bytes 1277960 | tf_op jit(solution)/shard_map/ppermute | solution.py:705
  12.2 68.8 %collective-permute-start.10 = (bf16[128,2688]{0,1:T(8,128)(2,1)S(1)}, bf16[128,2688]{0,1:T(8,128)(2,1)S(1)}, u32[]{:S(2)}, u32[]{:S(2)}) collective-permute-start(bf16[128,2688]{0,1:T(8,128)(2,1)S(1)} %bitcast_dynamic-update-slice_fusion.1), channel_id=1, source_target_pairs={{0,6},{1,7},{2,4},{3,5},{4,0},{5,1},{6,2},{7,3},{8,14},{9,15},{10,... | collective-permute-start | bytes 2064392 | tf_op jit(solution)/shard_map/ppermute | solution.py:705
  12.2 68.7 %collective-permute-start.11 = (bf16[128,2688]{0,1:T(8,128)(2,1)S(1)}, bf16[128,2688]{0,1:T(8,128)(2,1)S(1)}, u32[]{:S(2)}, u32[]{:S(2)}) collective-permute-start(bf16[128,2688]{0,1:T(8,128)(2,1)S(1)} %bitcast_dynamic-update-slice_fusion.1), channel_id=1, source_target_pairs={{4,6},{5,7},{6,4},{7,5},{12,14},{13,15},{14,12},{15,13},{20,22},{2... | collective-permute-start | bytes 2064392 | tf_op jit(solution)/shard_map/ppermute | solution.py:705
  14.2 59.1 %collective-permute-start = (bf16[256,1024]{1,0:T(8,128)(2,1)}, bf16[256,1024]{1,0:T(8,128)(2,1)}, u32[]{:S(2)}, u32[]{:S(2)}) collective-permute-start(bf16[256,1024]{1,0:T(8,128)(2,1)} %param.20), channel_id=1, source_target_pairs={{2,4},{3,5},{4,2},{5,3},{10,12},{11,13},{12,10},{13,11},{18,20},{1... | collective-permute-start | bytes 1572872 | tf_op jit(solution)/shard_map/ppermute | solution.py:705
  51.6 27.2 %collective-permute-start.24 = (bf16[256,1024]{1,0:T(8,128)(2,1)S(1)}, bf16[256,1024]{1,0:T(8,128)(2,1)S(1)}, u32[]{:S(2)}, u32[]{:S(2)}) collective-permute-start(bf16[256,1024]{1,0:T(8,128)(2,1)S(1)} %copy-done.30), channel_id=1, source_target_pairs={{2,4},{3,5},{4,2},{5,3},{10,12},{11,13},{12,10},{13,11},{18,20},{1... | collective-permute-start | bytes 1572872 | tf_op jit(solution)/shard_map/ppermute | solution.py:705
  55.2 36.3 %collective-permute-start.6 = (bf16[256,1664]{1,0:T(8,128)(2,1)S(1)}, bf16[256,1664]{1,0:T(8,128)(2,1)S(1)}, u32[]{:S(2)}, u32[]{:S(2)}) collective-permute-start(bf16[256,1664]{1,0:T(8,128)(2,1)S(1)} %pad_maximum_fusion.8), channel_id=1, source_target_pairs={{0,8},{1,9},{2,10},{3,11},{4,12},{5,13},{6,14},{7,15},{8,0},{9,1},... | collective-permute-start | bytes 2555912 | tf_op jit(solution)/shard_map/ppermute | solution.py:705
  73.3 12.0 %collective-permute-start.7 = (bf16[256,1664]{1,0:T(8,128)(2,1)S(1)}, bf16[256,1664]{1,0:T(8,128)(2,1)S(1)}, u32[]{:S(2)}, u32[]{:S(2)}) collective-permute-start(bf16[256,1664]{1,0:T(8,128)(2,1)S(1)} %pad_maximum_fusion.8), channel_id=1, source_target_pairs={{0,16},{1,17},{2,18},{3,19},{4,20},{5,21},{6,22},{7,23},{8,24},{9,... | collective-permute-start | bytes 2555912 | tf_op jit(solution)/shard_map/ppermute | solution.py:705
  80.5 9.7 %collective-permute-start.1 = (bf16[256,1024]{1,0:T(8,128)(2,1)S(1)}, bf16[256,1024]{1,0:T(8,128)(2,1)S(1)}, u32[]{:S(2)}, u32[]{:S(2)}) collective-permute-start(bf16[256,1024]{1,0:T(8,128)(2,1)S(1)} %fusion.18), channel_id=1, source_target_pairs={{0,1},{1,0},{2,3},{3,2},{4,5},{5,4},{6,7},{7,6},{8,9},{9,8},{10,11... | collective-permute-start | bytes 1572872 | tf_op jit(solution)/shard_map/ppermute | solution.py:705
  81.0 44.1 %collective-permute-start.2 = (bf16[256,1024]{1,0:T(8,128)(2,1)S(1)}, bf16[256,1024]{1,0:T(8,128)(2,1)S(1)}, u32[]{:S(2)}, u32[]{:S(2)}) collective-permute-start(bf16[256,1024]{1,0:T(8,128)(2,1)S(1)} %fusion.18), channel_id=1, source_target_pairs={{0,4},{1,5},{2,6},{3,7},{4,0},{5,1},{6,2},{7,3},{8,12},{9,13},{10,... | collective-permute-start | bytes 1572872 | tf_op jit(solution)/shard_map/ppermute | solution.py:705
  81.2 42.6 %collective-permute-start.13 = (bf16[256,2688]{0,1:T(8,128)(2,1)S(1)}, bf16[256,2688]{0,1:T(8,128)(2,1)S(1)}, u32[]{:S(2)}, u32[]{:S(2)}) collective-permute-start(bf16[256,2688]{0,1:T(8,128)(2,1)S(1)} %pad_maximum_fusion.6), channel_id=1, source_target_pairs={{0,16},{1,17},{2,18},{3,19},{4,20},{5,21},{6,22},{7,23},{8,24},{9,... | collective-permute-start | bytes 4128776 | tf_op jit(solution)/shard_map/ppermute | solution.py:705
  85.4 11.9 %collective-permute-start.8 = (bf16[128,1664]{1,0:T(8,128)(2,1)S(1)}, bf16[128,1664]{1,0:T(8,128)(2,1)S(1)}, u32[]{:S(2)}, u32[]{:S(2)}) collective-permute-start(bf16[128,1664]{1,0:T(8,128)(2,1)S(1)} %slice.564), channel_id=1, source_target_pairs={{0,8},{1,9},{2,10},{3,11},{4,12},{5,13},{6,14},{7,15},{8,0},{9,1},... | collective-permute-start | bytes 1277960 | tf_op jit(solution)/shard_map/ppermute | solution.py:705
  90.3 63.5 %collective-permute-start.12 = (bf16[256,2688]{0,1:T(8,128)(2,1)S(1)}, bf16[256,2688]{0,1:T(8,128)(2,1)S(1)}, u32[]{:S(2)}, u32[]{:S(2)}) collective-permute-start(bf16[256,2688]{0,1:T(8,128)(2,1)S(1)} %pad_maximum_fusion.6), channel_id=1, source_target_pairs={{0,8},{1,9},{2,10},{3,11},{4,12},{5,13},{6,14},{7,15},{8,0},{9,1},... | collective-permute-start | bytes 4128776 | tf_op jit(solution)/shard_map/ppermute | solution.py:705
  91.5 34.9 %collective-permute-start.3 = (bf16[256,1024]{1,0:T(8,128)(2,1)S(1)}, bf16[256,1024]{1,0:T(8,128)(2,1)S(1)}, u32[]{:S(2)}, u32[]{:S(2)}) collective-permute-start(bf16[256,1024]{1,0:T(8,128)(2,1)S(1)} %collective-permute-done.1), channel_id=1, source_target_pairs={{0,4},{1,5},{2,6},{3,7},{4,0},{5,1},{6,2},{7,3},{8,12},{9,13},{10,... | collective-permute-start | bytes 1572872 | tf_op jit(solution)/shard_map/ppermute | solution.py:705
  97.3 26.5 %collective-permute-start.9 = (bf16[128,1664]{1,0:T(8,128)(2,1)S(1)}, bf16[128,1664]{1,0:T(8,128)(2,1)S(1)}, u32[]{:S(2)}, u32[]{:S(2)}) collective-permute-start(bf16[128,1664]{1,0:T(8,128)(2,1)S(1)} %slice.565), channel_id=1, source_target_pairs={{0,16},{1,17},{2,18},{3,19},{4,20},{5,21},{6,22},{7,23},{8,24},{9,... | collective-permute-start | bytes 1277960 | tf_op jit(solution)/shard_map/ppermute | solution.py:705
  123.8 49.0 %collective-permute-start.25 = (bf16[256,1024]{1,0:T(8,128)(2,1)S(1)}, bf16[256,1024]{1,0:T(8,128)(2,1)}, u32[]{:S(2)}, u32[]{:S(2)}) collective-permute-start(bf16[256,1024]{1,0:T(8,128)(2,1)S(1)} %pad_maximum_fusion.15), channel_id=1, source_target_pairs={{0,1},{1,0},{2,3},{3,2},{4,5},{5,4},{6,7},{7,6},{8,9},{9,8},{10,11... | collective-permute-start | bytes 1572872 | tf_op jit(solution)/shard_map/ppermute | solution.py:705
  123.8 85.0 %collective-permute-start.26 = (bf16[256,1024]{1,0:T(8,128)(2,1)S(1)}, bf16[256,1024]{1,0:T(8,128)(2,1)}, u32[]{:S(2)}, u32[]{:S(2)}) collective-permute-start(bf16[256,1024]{1,0:T(8,128)(2,1)S(1)} %pad_maximum_fusion.15), channel_id=1, source_target_pairs={{0,4},{1,5},{2,6},{3,7},{4,0},{5,1},{6,2},{7,3},{8,12},{9,13},{10,... | collective-permute-start | bytes 1572872 | tf_op jit(solution)/shard_map/ppermute | solution.py:705
  125.1 30.2 %collective-permute-start.14 = (bf16[128,2688]{0,1:T(8,128)(2,1)S(1)}, bf16[128,2688]{0,1:T(8,128)(2,1)S(1)}, u32[]{:S(2)}, u32[]{:S(2)}) collective-permute-start(bf16[128,2688]{0,1:T(8,128)(2,1)S(1)} %slice.570), channel_id=1, source_target_pairs={{0,8},{1,9},{2,10},{3,11},{4,12},{5,13},{6,14},{7,15},{8,0},{9,1},... | collective-permute-start | bytes 2064392 | tf_op jit(solution)/shard_map/ppermute | solution.py:705
  153.9 16.7 %collective-permute-start.15 = (bf16[128,2688]{0,1:T(8,128)(2,1)S(1)}, bf16[128,2688]{0,1:T(8,128)(2,1)S(1)}, u32[]{:S(2)}, u32[]{:S(2)}) collective-permute-start(bf16[128,2688]{0,1:T(8,128)(2,1)S(1)} %slice.572), channel_id=1, source_target_pairs={{0,16},{1,17},{2,18},{3,19},{4,20},{5,21},{6,22},{7,23},{8,24},{9,... | collective-permute-start | bytes 2064392 | tf_op jit(solution)/shard_map/ppermute | solution.py:705
  171.4 3.5 collective-permute-start.16
  172.8 36.0 %collective-permute-start.27 = (bf16[256,1024]{1,0:T(8,128)(2,1)}, bf16[256,1024]{1,0:T(8,128)(2,1)S(1)}, u32[]{:S(2)}, u32[]{:S(2)}) collective-permute-start(bf16[256,1024]{1,0:T(8,128)(2,1)} %collective-permute-done.25), channel_id=1, source_target_pairs={{0,4},{1,5},{2,6},{3,7},{4,0},{5,1},{6,2},{7,3},{8,12},{9,13},{10,... | collective-permute-start | bytes 1572872 | tf_op jit(solution)/shard_map/ppermute | solution.py:705
  175.7 13.2 %collective-permute-start.17 = (bf16[256,1024]{1,0:T(8,128)(2,1)S(1)}, bf16[256,1024]{1,0:T(8,128)(2,1)S(1)}, u32[]{:S(2)}, u32[]{:S(2)}) collective-permute-start(bf16[256,1024]{1,0:T(8,128)(2,1)S(1)} %slice.1120), channel_id=1, source_target_pairs={{0,1},{1,0},{2,3},{3,2},{4,5},{5,4},{6,7},{7,6},{8,9},{9,8},{10,11... | collective-permute-start | bytes 1572872 | tf_op jit(solution)/shard_map/ppermute | solution.py:705
  189.4 12.3 %collective-permute-start.18 = (bf16[256,1024]{1,0:T(8,128)(2,1)S(1)}, bf16[256,1024]{1,0:T(8,128)(2,1)S(1)}, u32[]{:S(2)}, u32[]{:S(2)}) collective-permute-start(bf16[256,1024]{1,0:T(8,128)(2,1)S(1)} %multiply_convert_fusion.3), channel_id=1, source_target_pairs={{0,1},{1,0},{2,3},{3,2},{4,5},{5,4},{6,7},{7,6},{8,9},{9,8},{10,11... | collective-permute-start | bytes 1572872 | tf_op jit(solution)/shard_map/ppermute | solution.py:705
  190.6 13.4 %collective-permute-start.19 = (bf16[256,1024]{1,0:T(8,128)(2,1)S(1)}, bf16[256,1024]{1,0:T(8,128)(2,1)S(1)}, u32[]{:S(2)}, u32[]{:S(2)}) collective-permute-start(bf16[256,1024]{1,0:T(8,128)(2,1)S(1)} %multiply_convert_fusion.3), channel_id=1, source_target_pairs={{0,4},{1,5},{2,6},{3,7},{4,0},{5,1},{6,2},{7,3},{8,12},{9,13},{10,... | collective-permute-start | bytes 1572872 | tf_op jit(solution)/shard_map/ppermute | solution.py:705
  201.7 3.6 collective-permute-start.20
  219.2 11.1 %collective-permute-start.59 = (bf16[128,704]{0,1:T(8,128)(2,1)S(1)}, bf16[128,704]{0,1:T(8,128)(2,1)S(1)}, u32[]{:S(2)}, u32[]{:S(2)}) collective-permute-start(bf16[128,704]{0,1:T(8,128)(2,1)S(1)} %get-tuple-element.90), channel_id=1, source_target_pairs={{0,16},{1,17},{2,18},{3,19},{4,20},{5,21},{6,22},{7,23},{8,24},{9,... | collective-permute-start | bytes 540680 | tf_op jit(solution)/shard_map/ppermute | solution.py:705
  220.5 9.9 %collective-permute-start.61 = (bf16[128,704]{0,1:T(8,128)(2,1)S(1)}, bf16[128,704]{0,1:T(8,128)(2,1)S(1)}, u32[]{:S(2)}, u32[]{:S(2)}) collective-permute-start(bf16[128,704]{0,1:T(8,128)(2,1)S(1)} %get-tuple-element.89), channel_id=1, source_target_pairs={{0,8},{1,9},{2,10},{3,11},{4,12},{5,13},{6,14},{7,15},{8,0},{9,1},... | collective-permute-start | bytes 540680 | tf_op jit(solution)/shard_map/ppermute | solution.py:705
  226.3 9.1 %collective-permute-start.53 = (bf16[128,1408]{1,0:T(8,128)(2,1)S(1)}, bf16[128,1408]{1,0:T(8,128)(2,1)S(1)}, u32[]{:S(2)}, u32[]{:S(2)}) collective-permute-start(bf16[128,1408]{1,0:T(8,128)(2,1)S(1)} %get-tuple-element.84), channel_id=1, source_target_pairs={{0,16},{1,17},{2,18},{3,19},{4,20},{5,21},{6,22},{7,23},{8,24},{9,... | collective-permute-start | bytes 1081352 | tf_op jit(solution)/shard_map/ppermute | solution.py:705
  226.5 9.0 %collective-permute-start.55 = (bf16[128,1408]{1,0:T(8,128)(2,1)S(1)}, bf16[128,1408]{1,0:T(8,128)(2,1)S(1)}, u32[]{:S(2)}, u32[]{:S(2)}) collective-permute-start(bf16[128,1408]{1,0:T(8,128)(2,1)S(1)} %get-tuple-element.83), channel_id=1, source_target_pairs={{0,8},{1,9},{2,10},{3,11},{4,12},{5,13},{6,14},{7,15},{8,0},{9,1},... | collective-permute-start | bytes 1081352 | tf_op jit(solution)/shard_map/ppermute | solution.py:705
  228.8 31.9 %collective-permute-start.21 = (bf16[512,1024]{1,0:T(8,128)(2,1)S(1)}, bf16[512,1024]{1,0:T(8,128)(2,1)S(1)}, u32[]{:S(2)}, u32[]{:S(2)}) collective-permute-start(bf16[512,1024]{1,0:T(8,128)(2,1)S(1)} %convolution_convert_fusion.6), channel_id=1, source_target_pairs={{0,4},{1,5},{2,6},{3,7},{4,0},{5,1},{6,2},{7,3},{8,12},{9,13},{10,... | collective-permute-start | bytes 3145736 | tf_op jit(solution)/shard_map/ppermute | solution.py:705
  230.3 31.5 %collective-permute-start.28 = (bf16[512,1024]{1,0:T(8,128)(2,1)S(1)}, bf16[512,1024]{1,0:T(8,128)(2,1)S(1)}, u32[]{:S(2)}, u32[]{:S(2)}) collective-permute-start(bf16[512,1024]{1,0:T(8,128)(2,1)S(1)} %convolution_convert_fusion.5), channel_id=1, source_target_pairs={{0,4},{1,5},{2,6},{3,7},{4,0},{5,1},{6,2},{7,3},{8,12},{9,13},{10,... | collective-permute-start | bytes 3145736 | tf_op jit(solution)/shard_map/ppermute | solution.py:705
  230.6 12.4 %collective-permute-start.60 = (bf16[256,704]{0,1:T(8,128)(2,1)S(1)}, bf16[256,704]{0,1:T(8,128)(2,1)S(1)}, u32[]{:S(2)}, u32[]{:S(2)}) collective-permute-start(bf16[256,704]{0,1:T(8,128)(2,1)S(1)} %pad_maximum_fusion.16), channel_id=1, source_target_pairs={{0,8},{1,9},{2,10},{3,11},{4,12},{5,13},{6,14},{7,15},{8,0},{9,1},... | collective-permute-start | bytes 1081352 | tf_op jit(solution)/shard_map/ppermute | solution.py:705
  235.4 8.2 %collective-permute-start.62 = (bf16[256,704]{0,1:T(8,128)(2,1)S(1)}, bf16[256,704]{0,1:T(8,128)(2,1)S(1)}, u32[]{:S(2)}, u32[]{:S(2)}) collective-permute-start(bf16[256,704]{0,1:T(8,128)(2,1)S(1)} %pad_maximum_fusion.17), channel_id=1, source_target_pairs={{0,16},{1,17},{2,18},{3,19},{4,20},{5,21},{6,22},{7,23},{8,24},{9,... | collective-permute-start | bytes 1081352 | tf_op jit(solution)/shard_map/ppermute | solution.py:705
  235.8 29.4 %collective-permute-start.54 = (bf16[256,1408]{1,0:T(8,128)(2,1)S(1)}, bf16[256,1408]{1,0:T(8,128)(2,1)S(1)}, u32[]{:S(2)}, u32[]{:S(2)}) collective-permute-start(bf16[256,1408]{1,0:T(8,128)(2,1)S(1)} %pad_maximum_fusion.11), channel_id=1, source_target_pairs={{0,8},{1,9},{2,10},{3,11},{4,12},{5,13},{6,14},{7,15},{8,0},{9,1},... | collective-permute-start | bytes 2162696 | tf_op jit(solution)/shard_map/ppermute | solution.py:705
  243.8 9.6 %collective-permute-start.63 = (bf16[128,704]{0,1:T(8,128)(2,1)S(1)}, bf16[128,704]{0,1:T(8,128)(2,1)S(1)}, u32[]{:S(2)}, u32[]{:S(2)}) collective-permute-start(bf16[128,704]{0,1:T(8,128)(2,1)S(1)} %get-tuple-element.131), channel_id=1, source_target_pairs={{0,4},{1,5},{2,6},{3,7},{4,2},{5,3},{6,0},{7,1},{8,12},{9,13},{10,... | collective-permute-start | bytes 540680 | tf_op jit(solution)/shard_map/ppermute | solution.py:705
  250.9 9.0 %collective-permute-start.64 = (bf16[128,704]{0,1:T(8,128)(2,1)S(1)}, bf16[128,704]{0,1:T(8,128)(2,1)S(1)}, u32[]{:S(2)}, u32[]{:S(2)}) collective-permute-start(bf16[128,704]{0,1:T(8,128)(2,1)S(1)} %get-tuple-element.130), channel_id=1, source_target_pairs={{4,6},{5,7},{6,4},{7,5},{12,14},{13,15},{14,12},{15,13},{20,22},{2... | collective-permute-start | bytes 540680 | tf_op jit(solution)/shard_map/ppermute | solution.py:705
  253.3 16.4 %collective-permute-start.56 = (bf16[256,1408]{1,0:T(8,128)(2,1)S(1)}, bf16[256,1408]{1,0:T(8,128)(2,1)S(1)}, u32[]{:S(2)}, u32[]{:S(2)}) collective-permute-start(bf16[256,1408]{1,0:T(8,128)(2,1)S(1)} %pad_maximum_fusion.12), channel_id=1, source_target_pairs={{0,16},{1,17},{2,18},{3,19},{4,20},{5,21},{6,22},{7,23},{8,24},{9,... | collective-permute-start | bytes 2162696 | tf_op jit(solution)/shard_map/ppermute | solution.py:705
  261.8 30.0 %collective-permute-start.22 = (bf16[256,1024]{1,0:T(8,128)(2,1)S(1)}, bf16[256,1024]{1,0:T(8,128)(2,1)S(1)}, u32[]{:S(2)}, u32[]{:S(2)}) collective-permute-start(bf16[256,1024]{1,0:T(8,128)(2,1)S(1)} %slice.1119), channel_id=1, source_target_pairs={{0,1},{1,0},{2,3},{3,2},{4,5},{5,4},{6,7},{7,6},{8,9},{9,8},{10,11... | collective-permute-start | bytes 1572872 | tf_op jit(solution)/shard_map/ppermute | solution.py:705
  263.7 27.6 %collective-permute-start.29 = (bf16[256,1024]{1,0:T(8,128)(2,1)S(1)}, bf16[256,1024]{1,0:T(8,128)(2,1)S(1)}, u32[]{:S(2)}, u32[]{:S(2)}) collective-permute-start(bf16[256,1024]{1,0:T(8,128)(2,1)S(1)} %slice.1118), channel_id=1, source_target_pairs={{0,1},{1,0},{2,3},{3,2},{4,5},{5,4},{6,7},{7,6},{8,9},{9,8},{10,11... | collective-permute-start | bytes 1572872 | tf_op jit(solution)/shard_map/ppermute | solution.py:705
  270.1 32.5 %collective-permute-start.57 = (bf16[128,1408]{1,0:T(8,128)(2,1)S(1)}, bf16[128,1408]{1,0:T(8,128)(2,1)S(1)}, u32[]{:S(2)}, u32[]{:S(2)}) collective-permute-start(bf16[128,1408]{1,0:T(8,128)(2,1)S(1)} %get-tuple-element.115), channel_id=1, source_target_pairs={{0,4},{1,5},{2,6},{3,7},{4,2},{5,3},{6,0},{7,1},{8,12},{9,13},{10,... | collective-permute-start | bytes 1081352 | tf_op jit(solution)/shard_map/ppermute | solution.py:705
  274.6 28.0 %collective-permute-start.58 = (bf16[128,1408]{1,0:T(8,128)(2,1)S(1)}, bf16[128,1408]{1,0:T(8,128)(2,1)S(1)}, u32[]{:S(2)}, u32[]{:S(2)}) collective-permute-start(bf16[128,1408]{1,0:T(8,128)(2,1)S(1)} %get-tuple-element.114), channel_id=1, source_target_pairs={{4,6},{5,7},{6,4},{7,5},{12,14},{13,15},{14,12},{15,13},{20,22},{2... | collective-permute-start | bytes 1081352 | tf_op jit(solution)/shard_map/ppermute | solution.py:705
  293.5 17.6 %collective-permute-start.30 = (bf16[256,1024]{1,0:T(8,128)(2,1)}, bf16[256,1024]{1,0:T(8,128)(2,1)}, u32[]{:S(2)}, u32[]{:S(2)}) collective-permute-start(bf16[256,1024]{1,0:T(8,128)(2,1)} %get-tuple-element.64), channel_id=1, source_target_pairs={{0,1},{1,0},{2,3},{3,2},{4,5},{5,4},{6,7},{7,6},{8,9},{9,8},{10,11... | collective-permute-start | bytes 1572872 | tf_op jit(solution)/shard_map/ppermute | solution.py:705
  294.5 22.0 %collective-permute-start.23 = (bf16[256,1024]{1,0:T(8,128)(2,1)}, bf16[256,1024]{1,0:T(8,128)(2,1)}, u32[]{:S(2)}, u32[]{:S(2)}) collective-permute-start(bf16[256,1024]{1,0:T(8,128)(2,1)} %pad_maximum_fusion.14), channel_id=1, source_target_pairs={{2,4},{3,5},{4,2},{5,3},{10,12},{11,13},{12,10},{13,11},{18,20},{1... | collective-permute-start | bytes 1572872 | tf_op jit(solution)/shard_map/ppermute | solution.py:705
  302.8 15.8 %collective-permute-start.31 = (bf16[256,1024]{1,0:T(8,128)(2,1)}, bf16[256,1024]{1,0:T(8,128)(2,1)}, u32[]{:S(2)}, u32[]{:S(2)}) collective-permute-start(bf16[256,1024]{1,0:T(8,128)(2,1)} %get-tuple-element.64), channel_id=1, source_target_pairs={{0,4},{1,5},{2,6},{3,7},{4,0},{5,1},{6,2},{7,3},{8,12},{9,13},{10,... | collective-permute-start | bytes 1572872 | tf_op jit(solution)/shard_map/ppermute | solution.py:705
  311.1 7.5 %collective-permute-start.32 = (bf16[256,1024]{1,0:T(8,128)(2,1)}, bf16[256,1024]{1,0:T(8,128)(2,1)}, u32[]{:S(2)}, u32[]{:S(2)}) collective-permute-start(bf16[256,1024]{1,0:T(8,128)(2,1)} %collective-permute-done.30), channel_id=1, source_target_pairs={{0,4},{1,5},{2,6},{3,7},{4,0},{5,1},{6,2},{7,3},{8,12},{9,13},{10,... | collective-permute-start | bytes 1572872 | tf_op jit(solution)/shard_map/ppermute | solution.py:705
  321.9 50.7 %collective-permute-start.47 = (bf16[128,512]{1,0:T(8,128)(2,1)S(1)}, bf16[128,512]{1,0:T(8,128)(2,1)S(1)}, u32[]{:S(2)}, u32[]{:S(2)}) collective-permute-start(bf16[128,512]{1,0:T(8,128)(2,1)S(1)} %get-tuple-element.96), channel_id=1, source_target_pairs={{0,16},{1,17},{2,18},{3,19},{4,20},{5,21},{6,22},{7,23},{8,24},{9,... | collective-permute-start | bytes 393224 | tf_op jit(solution)/shard_map/ppermute | solution.py:705
  322.0 50.6 %collective-permute-start.49 = (bf16[128,512]{1,0:T(8,128)(2,1)S(1)}, bf16[128,512]{1,0:T(8,128)(2,1)S(1)}, u32[]{:S(2)}, u32[]{:S(2)}) collective-permute-start(bf16[128,512]{1,0:T(8,128)(2,1)S(1)} %get-tuple-element.95), channel_id=1, source_target_pairs={{0,8},{1,9},{2,10},{3,11},{4,12},{5,13},{6,14},{7,15},{8,0},{9,1},... | collective-permute-start | bytes 393224 | tf_op jit(solution)/shard_map/ppermute | solution.py:705
  369.2 26.9 %collective-permute-start.41 = (bf16[128,1664]{1,0:T(8,128)(2,1)S(1)}, bf16[128,1664]{1,0:T(8,128)(2,1)S(1)}, u32[]{:S(2)}, u32[]{:S(2)}) collective-permute-start(bf16[128,1664]{1,0:T(8,128)(2,1)S(1)} %get-tuple-element.78), channel_id=1, source_target_pairs={{0,16},{1,17},{2,18},{3,19},{4,20},{5,21},{6,22},{7,23},{8,24},{9,... | collective-permute-start | bytes 1277960 | tf_op jit(solution)/shard_map/ppermute | solution.py:705
  370.6 25.5 %collective-permute-start.43 = (bf16[128,1664]{1,0:T(8,128)(2,1)S(1)}, bf16[128,1664]{1,0:T(8,128)(2,1)S(1)}, u32[]{:S(2)}, u32[]{:S(2)}) collective-permute-start(bf16[128,1664]{1,0:T(8,128)(2,1)S(1)} %get-tuple-element.77), channel_id=1, source_target_pairs={{0,8},{1,9},{2,10},{3,11},{4,12},{5,13},{6,14},{7,15},{8,0},{9,1},... | collective-permute-start | bytes 1277960 | tf_op jit(solution)/shard_map/ppermute | solution.py:705
  371.1 30.6 %collective-permute-start.33 = (bf16[512,1024]{1,0:T(8,128)(2,1)}, bf16[512,1024]{1,0:T(8,128)(2,1)}, u32[]{:S(2)}, u32[]{:S(2)}) collective-permute-start(bf16[512,1024]{1,0:T(8,128)(2,1)} %fusion.11), channel_id=1, source_target_pairs={{0,4},{1,5},{2,6},{3,7},{4,0},{5,1},{6,2},{7,3},{8,12},{9,13},{10,... | collective-permute-start | bytes 3145736 | tf_op jit(solution)/shard_map/ppermute | solution.py:705
  372.7 13.5 %collective-permute-start.48 = (bf16[256,512]{1,0:T(8,128)(2,1)S(1)}, bf16[256,512]{1,0:T(8,128)(2,1)S(1)}, u32[]{:S(2)}, u32[]{:S(2)}) collective-permute-start(bf16[256,512]{1,0:T(8,128)(2,1)S(1)} %pad_maximum_fusion.24), channel_id=1, source_target_pairs={{0,8},{1,9},{2,10},{3,11},{4,12},{5,13},{6,14},{7,15},{8,0},{9,1},... | collective-permute-start | bytes 786440 | tf_op jit(solution)/shard_map/ppermute | solution.py:705
  374.0 12.3 %collective-permute-start.50 = (bf16[256,512]{1,0:T(8,128)(2,1)S(1)}, bf16[256,512]{1,0:T(8,128)(2,1)S(1)}, u32[]{:S(2)}, u32[]{:S(2)}) collective-permute-start(bf16[256,512]{1,0:T(8,128)(2,1)S(1)} %pad_maximum_fusion.25), channel_id=1, source_target_pairs={{0,16},{1,17},{2,18},{3,19},{4,20},{5,21},{6,22},{7,23},{8,24},{9,... | collective-permute-start | bytes 786440 | tf_op jit(solution)/shard_map/ppermute | solution.py:705
  386.4 12.7 %collective-permute-start.51 = (bf16[128,512]{1,0:T(8,128)(2,1)S(1)}, bf16[128,512]{1,0:T(8,128)(2,1)S(1)}, u32[]{:S(2)}, u32[]{:S(2)}) collective-permute-start(bf16[128,512]{1,0:T(8,128)(2,1)S(1)} %get-tuple-element.133), channel_id=1, source_target_pairs={{0,4},{1,5},{2,6},{3,7},{4,2},{5,3},{6,0},{7,1},{8,12},{9,13},{10,... | collective-permute-start | bytes 393224 | tf_op jit(solution)/shard_map/ppermute | solution.py:705
  394.2 6.6 %collective-permute-start.52 = (bf16[128,512]{1,0:T(8,128)(2,1)S(1)}, bf16[128,512]{1,0:T(8,128)(2,1)S(1)}, u32[]{:S(2)}, u32[]{:S(2)}) collective-permute-start(bf16[128,512]{1,0:T(8,128)(2,1)S(1)} %get-tuple-element.132), channel_id=1, source_target_pairs={{4,6},{5,7},{6,4},{7,5},{12,14},{13,15},{14,12},{15,13},{20,22},{2... | collective-permute-start | bytes 393224 | tf_op jit(solution)/shard_map/ppermute | solution.py:705
  396.4 14.8 %collective-permute-start.42 = (bf16[256,1664]{1,0:T(8,128)(2,1)S(1)}, bf16[256,1664]{1,0:T(8,128)(2,1)}, u32[]{:S(2)}, u32[]{:S(2)}) collective-permute-start(bf16[256,1664]{1,0:T(8,128)(2,1)S(1)} %pad_maximum_fusion.9), channel_id=1, source_target_pairs={{0,8},{1,9},{2,10},{3,11},{4,12},{5,13},{6,14},{7,15},{8,0},{9,1},... | collective-permute-start | bytes 2555912 | tf_op jit(solution)/shard_map/ppermute | solution.py:705
  396.8 15.1 %collective-permute-start.44 = (bf16[256,1664]{1,0:T(8,128)(2,1)S(1)}, bf16[256,1664]{1,0:T(8,128)(2,1)}, u32[]{:S(2)}, u32[]{:S(2)}) collective-permute-start(bf16[256,1664]{1,0:T(8,128)(2,1)S(1)} %pad_maximum_fusion.10), channel_id=1, source_target_pairs={{0,16},{1,17},{2,18},{3,19},{4,20},{5,21},{6,22},{7,23},{8,24},{9,... | collective-permute-start | bytes 2555912 | tf_op jit(solution)/shard_map/ppermute | solution.py:705
  406.6 15.7 %collective-permute-start.34 = (bf16[256,1024]{1,0:T(8,128)(2,1)S(1)}, bf16[256,1024]{1,0:T(8,128)(2,1)S(1)}, u32[]{:S(2)}, u32[]{:S(2)}) collective-permute-start(bf16[256,1024]{1,0:T(8,128)(2,1)S(1)} %slice.1117), channel_id=1, source_target_pairs={{0,1},{1,0},{2,3},{3,2},{4,5},{5,4},{6,7},{7,6},{8,9},{9,8},{10,11... | collective-permute-start | bytes 1572872 | tf_op jit(solution)/shard_map/ppermute | solution.py:705
  414.9 14.3 %collective-permute-start.45 = (bf16[128,1664]{1,0:T(8,128)(2,1)}, bf16[128,1664]{1,0:T(8,128)(2,1)}, u32[]{:S(2)}, u32[]{:S(2)}) collective-permute-start(bf16[128,1664]{1,0:T(8,128)(2,1)} %get-tuple-element.111), channel_id=1, source_target_pairs={{0,4},{1,5},{2,6},{3,7},{4,2},{5,3},{6,0},{7,1},{8,12},{9,13},{10,... | collective-permute-start | bytes 1277960 | tf_op jit(solution)/shard_map/ppermute | solution.py:705
  418.1 33.1 %collective-permute-start.46 = (bf16[128,1664]{1,0:T(8,128)(2,1)}, bf16[128,1664]{1,0:T(8,128)(2,1)}, u32[]{:S(2)}, u32[]{:S(2)}) collective-permute-start(bf16[128,1664]{1,0:T(8,128)(2,1)} %get-tuple-element.110), channel_id=1, source_target_pairs={{4,6},{5,7},{6,4},{7,5},{12,14},{13,15},{14,12},{15,13},{20,22},{2... | collective-permute-start | bytes 1277960 | tf_op jit(solution)/shard_map/ppermute | solution.py:705
  423.7 4.1 collective-permute-start.36
  425.6 42.5 %collective-permute-start.35 = (bf16[256,1024]{1,0:T(8,128)(2,1)S(1)}, bf16[256,1024]{1,0:T(8,128)(2,1)S(1)}, u32[]{:S(2)}, u32[]{:S(2)}) collective-permute-start(bf16[256,1024]{1,0:T(8,128)(2,1)S(1)} %fusion.31), channel_id=1, source_target_pairs={{2,4},{3,5},{4,2},{5,3},{10,12},{11,13},{12,10},{13,11},{18,20},{1... | collective-permute-start | bytes 1572872 | tf_op jit(solution)/shard_map/ppermute | solution.py:705
  427.9 24.6 %collective-permute-start.37 = (f32[18704]{0:T(1024)S(1)}, f32[18704]{0:T(1024)S(1)}, u32[]{:S(2)}, u32[]{:S(2)}) collective-permute-start(f32[18704]{0:T(1024)S(1)} %add.179), channel_id=1, source_target_pairs={{0,8},{1,9},{2,10},{3,11},{4,12},{5,13},{6,14},{7,15},{8,0},{9,1},... | collective-permute-start | bytes 224456 | tf_op jit(solution)/shard_map/ppermute | solution.py:705
  455.9 4.2 collective-permute-start.39
  460.0 4.3 collective-permute-start.40
  (50 other events, 1124.0 us)
